TPU v7x, 32 devices: a whole 2x2x4 slice. The times are simulated.
32 devices in a mesh: dp: 4 (over y, x), fsdp: 8 (over z, core).
Axes of the slice: x: 2, y: 2, z: 4, core: 2. Of those that a mesh axis runs over, the one named last changes fastest.
Arguments:
- tokens: bfloat16 [32, 512, 768], P(('dp', 'fsdp')), may hold values from -6 to 6
- lengths: int32 [32], P(('dp', 'fsdp')), may hold values from 30 to 512, as said below
- cotangent: bfloat16 [32, 512, 768], P(('dp', 'fsdp')), may hold values from -6 to 6
- query_weight: bfloat16 [768, 768], P('fsdp'), may hold values from -0.21875 to 0.21875
- query_bias: bfloat16 [768], P('fsdp'), may hold values from -3 to 3
- key_weight: bfloat16 [768, 768], P('fsdp'), may hold values from -0.21875 to 0.21875
- value_weight: bfloat16 [768, 768], P('fsdp'), may hold values from -0.21875 to 0.21875
- value_bias: bfloat16 [768], P('fsdp'), may hold values from -3 to 3
- output_weight: bfloat16 [768, 768], P('fsdp'), may hold values from -3.5 to 3.5
- output_bias: bfloat16 [768], P('fsdp'), may hold values from -3 to 3
- first_gain: bfloat16 [768], P('fsdp'), may hold values from 0.25 to 1.75
- first_shift: bfloat16 [768], P('fsdp'), may hold values from -3 to 3
- inner_weight: bfloat16 [768, 3072], P('fsdp'), may hold values from -0.21875 to 0.21875
- inner_bias: bfloat16 [3072], P('fsdp'), may hold values from -3 to 3
- outer_weight: bfloat16 [3072, 768], P('fsdp'), may hold values from -0.109375 to 0.109375
- outer_bias: bfloat16 [768], P('fsdp'), may hold values from -3 to 3
- second_gain: bfloat16 [768], P('fsdp'), may hold values from 0.25 to 1.75
- second_shift: bfloat16 [768], P('fsdp'), may hold values from -3 to 3
Outputs:
- block_output: bfloat16 [32, 512, 768], P(('dp', 'fsdp'))
- input_grad: float32 [32, 512, 768], P(('dp', 'fsdp'))
- query_weight_grad: float32 [768, 768], P('fsdp')
- query_bias_grad: float32 [768], P('fsdp')
- key_weight_grad: float32 [768, 768], P('fsdp')
- value_weight_grad: float32 [768, 768], P('fsdp')
- value_bias_grad: float32 [768], P('fsdp')
- output_weight_grad: float32 [768, 768], P('fsdp')
- output_bias_grad: float32 [768], P('fsdp')
- first_gain_grad: float32 [768], P('fsdp')
- first_shift_grad: float32 [768], P('fsdp')
- inner_weight_grad: float32 [768, 3072], P('fsdp')
- inner_bias_grad: float32 [3072], P('fsdp')
- outer_weight_grad: float32 [3072, 768], P('fsdp')
- outer_bias_grad: float32 [768], P('fsdp')
- second_gain_grad: float32 [768], P('fsdp')
- second_shift_grad: float32 [768], P('fsdp')
Inputs may be any that keep to these rules, and one draw needn't show every extreme that they name: Document i holds its true tokens in slots 0 to lengths[i] - 1, the rest is padding; in every draw some document has exactly 512 and another exactly 30.
All inputs are finite; a program needn't handle non-finite values.
Results may differ from a plain program's by a relative error of at most 0.015.
Values may be sent and summed in bfloat16 or wider, within the bound.
No kernel may reach another device: no remote copies, remote signals or barrier semaphores. Data moves between devices by JAX's collectives and lax.ppermute only.
A program may use at most 192 MiB of HBM per device.

v0:
```python
import functools
import math

import jax
import jax.numpy as jnp
from jax import lax
from jax.experimental import pallas as pl
from jax.experimental.pallas import tpu as pltpu
from jax.sharding import PartitionSpec as P

F32 = jnp.float32
BF16 = jnp.bfloat16
HD = 64
MASKED = -1e30
SCALE = HD ** -0.5
EPSILON = 1e-12
ROOT_HALF = math.sqrt(0.5)
INV_ROOT_TWO_PI = 1.0 / math.sqrt(2.0 * math.pi)

VM = pl.BlockSpec(memory_space=pltpu.VMEM)
SM = pl.BlockSpec(memory_space=pltpu.SMEM)
HB = pl.BlockSpec(memory_space=pl.ANY)
FREE = pl.CostEstimate(flops=0, bytes_accessed=0, transcendentals=0)

LONG = pl.CostEstimate(flops=60_000_000_000, bytes_accessed=0, transcendentals=0)


def shape(*dims, dtype=BF16):
    return jax.ShapeDtypeStruct(dims, dtype)


def local(*dims, dtype=BF16):
    return pltpu.VMEM(dims, dtype)


def stay(*values):
    return tuple(pltpu.with_memory_space_constraint(v, pltpu.VMEM) for v in values)


def far_off(*values):
    return tuple(pltpu.with_memory_space_constraint(v, pltpu.HBM) for v in values)


def limit(mebibytes):
    return pltpu.CompilerParams(vmem_limit_bytes=mebibytes << 20)


def dot_nn(a, b):
    return lax.dot_general(a, b, (((1,), (0,)), ((), ())), preferred_element_type=F32)


def dot_nt(a, b):
    return lax.dot_general(a, b, (((1,), (1,)), ((), ())), preferred_element_type=F32)


def flip(value):
    return value.T


def column_sum(value):
    return jnp.sum(value.astype(F32), axis=0, keepdims=True)


def row_mean(value):
    return jnp.mean(value, axis=-1, keepdims=True)


def aligned(start, size):
    return pl.ds(pl.multiple_of(start, size), size)


class Pieces:
    def __init__(self, held, arrays, own, sibling, far, far_sibling, stacked, packs=()):
        self.held, self.arrays, self.own, self.sibling, self.packs = held, arrays, own, sibling, packs
        self.far, self.far_sibling, self.stacked = far, far_sibling, stacked

    def count(self):
        return len(self.own)

    def place(self, target, block, z_at, c_at, offset, rows):
        if self.stacked:
            return target.at[block, aligned_rows((2 * z_at + c_at) * 96 + offset, rows), :]
        return target.at[aligned_rows((2 * z_at + c_at) * 384 + block * 96 + offset, rows), :]

    def copies(self, held, me_ref, target, sems, base):
        z, c = me_ref[1], me_ref[2]
        done = []
        for block, (position, row, lane) in enumerate(self.own):
            where = self.place(target, block, z, c, 0, 96)
            source = held[position].at[pl.ds(row, 96), pl.ds(lane, 768)]
            done.append(pltpu.make_async_copy(source, where, sems.at[base + block]))
        return done

    def fill(self, refs, me_ref, target, rest=(0, 1, 2, 3)):
        i, z, c = me_ref[0], me_ref[1], me_ref[2]
        for block, (position, tile) in enumerate(self.sibling if 0 in rest else ()):
            self.place(target, block, z, 1 - c, 0, 96)[...] = refs[position][tile]
        for c_at, far in ((c, self.far), (1 - c, self.far_sibling)):
            for away in rest:
                parts = far[away]
                for position, tile, row, rows, offset in parts:

                    def copy(j, carry, position=position, tile=tile, row=row, rows=rows, offset=offset, away=away, c_at=c_at):
                        where = self.place(target, i ^ away, z ^ j, c_at, offset, rows)
                        where[...] = refs[position][tile + j - 1, row : row + rows, :]
                        return carry

                    lax.fori_loop(1, 4, copy, 0)

    def vectors(self, refs, me_ref, target):
        z, c = me_ref[1], me_ref[2]
        own, mine, other = (refs[n] for n in self.packs)
        for j in range(4):
            target[2 * (z ^ j) + c] = (mine[j - 1, 96:104, :] if j else own[96:104, :]).astype(F32)
            target[2 * (z ^ j) + 1 - c] = other[13, 8 * j : 8 * j + 8, :].astype(F32)


def bundle_body(group_count, held, me_ref, *refs):
    sources, near = refs[: len(held)], refs[len(held) : -2]
    out_ref, sems = refs[-2:]
    own = [(n, row, lane) for n, spots in enumerate(held) for row, lane in spots]
    loads = []
    for tile, (n, row, lane) in enumerate(own):
        source = sources[n].at[pl.ds(row, 96), pl.ds(lane, 768)]
        loads.append(pltpu.make_async_copy(source, out_ref.at[tile], sems.at[tile]))
    start_all(loads)
    tile = len(own)
    for away in range(3):
        for group in range(group_count):
            for j in range(3):
                out_ref[tile] = near[away * group_count + group][j, :96, :]
                tile += 1
    if group_count == 1:
        out_ref[tile, 0:8, :] = near[3][96:104, :]
        for j in range(3):
            out_ref[tile, 8 * j + 8 : 8 * j + 16, :] = near[0][j, 96:104, :]
        out_ref[tile, 32:, :] = jnp.zeros((64, 768), BF16)
    wait_all(loads)


def bundle(group_count, sources, held, near):
    own = sum(len(spots) for spots in held)
    tiles = own + 9 * group_count + (group_count == 1)
    return pl.pallas_call(
        functools.partial(bundle_body, group_count, held),
        out_shape=local(tiles, 96, 768),
        in_specs=[SM] + [HB] * len(sources) + [VM] * len(near),
        out_specs=VM,
        scratch_shapes=[pltpu.SemaphoreType.DMA((own,))],
        compiler_params=limit(2),
        cost_estimate=FREE,
        name="bundle",
    )(jnp.zeros((1,), jnp.int32), *far_off(*sources), *stay(*near))


def aligned_rows(start, rows):
    return pl.ds(pl.multiple_of(start, 16), rows)


class Whole:
    def __init__(self, held, arrays, spots, stacked):
        self.held, self.arrays, self.spots, self.stacked = held, arrays, spots, stacked

    def count(self):
        return len(self.spots)

    def copies(self, held, me_ref, target, sems, base):
        done = []
        for block, (position, row, lane) in enumerate(self.spots):
            where = target.at[block] if self.stacked else target.at[pl.ds(block * 768, 768), :]
            source = held[position].at[pl.ds(row, 768), pl.ds(lane, 768)]
            done.append(pltpu.make_async_copy(source, where, sems.at[base + block]))
        return done

    def fill(self, refs, me_ref, target, rest=()):
        pass

    def vectors(self, refs, me_ref, target):
        target[...] = refs[0][...].astype(F32)


def start_all(copies):
    for copy in copies:
        copy.start()


def wait_all(copies):
    for copy in copies:
        copy.wait()


def pair_masks(dims, axis):
    spot = lax.broadcasted_iota(jnp.int32, dims, axis)
    return spot < HD, spot >= HD


def keep(mask, value):
    return jnp.where(mask, value, jnp.zeros_like(value))


def attend_forward_body(group, part, me_ref, len_ref, x_ref, *refs):
    held, refs = refs[: len(group.held)], refs[len(group.held) :]
    sources = refs[: len(group.arrays)]
    q_ref, k_ref, v_ref, att_ref, left_ref, lse_ref, w_ref, vec_ref, ib_ref, packed, sems = refs[len(group.arrays) :]
    seq, width = x_ref.shape
    tile = min(512, seq)
    loads = group.copies(held, me_ref, w_ref, sems, 0)
    start_all(loads)
    group.fill(sources, me_ref, w_ref)
    group.vectors(sources, me_ref, packed)
    for f in range(packed.shape[0]):
        pack = packed[f]
        vec_ref[:, f * part : (f + 1) * part] = pack[:, :part]
        row, lane = divmod(f * 4 * part, width)
        ib_ref[row : row + 1, lane : lane + 4 * part] = pack[:1, 128 : 128 + 4 * part]
    for p in range(width // 128):
        left_ref[0, p * 128 : (p + 1) * 128, :] = flip(x_ref[:, p * 128 : (p + 1) * 128])
    wait_all(loads)

    def project(r, carry):
        rows = aligned(r * tile, tile)
        x = x_ref[rows, :]
        q_ref[rows, :] = (dot_nn(x, w_ref[0]) + vec_ref[0:1, :]).astype(BF16)
        k_ref[rows, :] = dot_nn(x, w_ref[1]).astype(BF16)
        v_ref[rows, :] = (dot_nn(x, w_ref[2]) + vec_ref[1:2, :]).astype(BF16)
        return carry

    lax.fori_loop(0, seq // tile, project, 0)
    length = len_ref[0]

    def pair(p, carry):
        lanes = aligned(p * 128, 128)
        k_pair = k_ref[:, lanes]
        q_t = (q_ref[:, lanes].astype(F32) * SCALE).T.astype(BF16)
        v_t = flip(v_ref[:, lanes])
        masks = pair_masks((128, seq), 0)
        allowed = lax.broadcasted_iota(jnp.int32, (seq, seq), 0) < length
        for e in range(2):
            s = dot_nn(k_pair, keep(masks[e], q_t))
            s = jnp.where(allowed, s, MASKED)
            top = jnp.max(s, axis=0, keepdims=True)
            p_t = jnp.exp(s - top)
            total = jnp.sum(p_t, axis=0, keepdims=True)
            o_t = dot_nn(v_t[e * HD : (e + 1) * HD, :], p_t.astype(BF16)) / total
            left_ref[1, aligned(p * 128 + e * HD, HD), :] = o_t.astype(BF16)
            lse_ref[pl.ds(p * 2 + e, 1), :] = top + jnp.log(total)
        att_ref[:, lanes] = flip(left_ref[1, aligned(p * 128, 128), :])
        return carry

    lax.fori_loop(0, width // 128, pair, 0, unroll=2)


def attend_forward(group, shards, blocks, me, length, x):
    seq, width = x.shape
    heads = width // HD
    return pl.pallas_call(
        functools.partial(attend_forward_body, group, width // shards),
        out_shape=(local(seq, width),) * 4
        + (local(2, width, seq), local(-(-heads // 8) * 8, seq, dtype=F32), local(4, width, width))
        + (local(8, width, dtype=F32), local(blocks, width, dtype=F32)),
        in_specs=[SM, SM, VM] + [HB] * len(group.held) + [VM] * len(group.arrays),
        out_specs=[VM] * 9,
        scratch_shapes=[pltpu.VMEM((shards, 8, width), F32), pltpu.SemaphoreType.DMA((group.count(),))],
        compiler_params=limit(10),
        cost_estimate=FREE,
        name="attend_forward",
    )(me, length, x, *far_off(*group.held), *stay(*group.arrays))


def attend_backward_body(first, last, len_ref, q_ref, k_ref, v_ref, do_ref, lse_ref, branch_ref, *refs):
    g_ref, sum_ref = refs[-2:]
    seq, width = q_ref.shape
    length = len_ref[0]

    def pair(p, carry):
        lanes = aligned(p * 128, 128)
        q_pair = (q_ref[:, lanes].astype(F32) * SCALE).astype(BF16)
        k_pair = k_ref[:, lanes]
        v_pair = v_ref[:, lanes]
        do_pair = do_ref[:, lanes]
        q_t = flip(q_pair)
        k_t = (k_pair.astype(F32) * SCALE).T.astype(BF16)
        do_t = flip(do_pair)
        sub_masks = pair_masks((128, seq), 0)
        lane_masks = pair_masks((seq, 128), 1)
        allowed = lax.broadcasted_iota(jnp.int32, (seq, seq), 0) < length
        dk = jnp.zeros((seq, 128), F32)
        dv = jnp.zeros((seq, 128), F32)
        dq_t = []
        for e in range(2):
            s = dot_nn(k_pair, keep(sub_masks[e], q_t))
            s = jnp.where(allowed, s, MASKED)
            p_t = jnp.exp(s - lse_ref[pl.ds(p * 2 + e, 1), :])
            dp = dot_nn(v_pair, keep(sub_masks[e], do_t))
            dv = dv + dot_nn(p_t.astype(BF16), keep(lane_masks[e], do_pair))
            t = p_t * dp
            row = jnp.sum(t, axis=0, keepdims=True)
            ds = (t - p_t * row).astype(BF16)
            dk = dk + dot_nn(ds, keep(lane_masks[e], q_pair))
            dq_t.append(dot_nn(k_t[e * HD : (e + 1) * HD, :], ds))
        dq = jnp.concatenate(dq_t, axis=0).T.astype(BF16)
        dv = dv.astype(BF16)
        g_ref[0, :, lanes] = dq
        g_ref[1, :, lanes] = dk.astype(BF16)
        g_ref[2, :, lanes] = dv
        g_ref[3, :, lanes] = branch_ref[:, lanes]
        sum_ref[0:1, lanes] = column_sum(dq)
        sum_ref[1:2, lanes] = column_sum(dv)
        return carry

    lax.fori_loop(first, last, pair, 0, unroll=2)


def attend_backward(first, last, length, q, k, v, do, lse, branch, before=()):
    seq, width = q.shape
    return pl.pallas_call(
        functools.partial(attend_backward_body, first, last),
        out_shape=(local(4, seq, width), local(8, width, dtype=F32)),
        in_specs=[SM] + [VM] * 6 + [HB] * len(before),
        out_specs=[VM] * 2,
        input_output_aliases={7 + n: n for n in range(len(before))},
        compiler_params=limit(10),
        cost_estimate=FREE,
        name="attend_backward",
    )(length, *stay(q, k, v, do, lse, branch, *before))


def gelu_parts(inner):
    cumulative = 0.5 * (1.0 + lax.erf(inner * ROOT_HALF))
    density = jnp.exp(-0.5 * inner * inner) * INV_ROOT_TWO_PI
    return inner * cumulative, cumulative + inner * density


def fill_body(group, early, me_ref, *refs):
    held, near = refs[: len(group.held)], refs[len(group.held) : len(group.held) + len(group.arrays)]
    if not early:
        group.fill(near, me_ref, refs[-1])
        return
    target, sems = refs[-2:]
    loads = group.copies(held, me_ref, target, sems, 0)
    start_all(loads)
    group.fill(near, me_ref, target)
    wait_all(loads)


def fill(group, me, *dims, before=None):
    early = before is None
    more = () if early else (before,)
    return pl.pallas_call(
        functools.partial(fill_body, group, early),
        out_shape=local(*dims),
        in_specs=[SM] + [HB] * len(group.held) + [VM] * len(group.arrays) + [HB] * len(more),
        out_specs=VM,
        scratch_shapes=[pltpu.SemaphoreType.DMA((group.count(),))] * early,
        input_output_aliases={} if early else {1 + len(group.held) + len(group.arrays): 0},
        compiler_params=limit(2),
        cost_estimate=FREE,
        name="fill",
    )(me, *far_off(*group.held), *stay(*group.arrays, *more))


def middle_forward_body(
    len_ref,
    x_ref,
    att_ref,
    cot_ref,
    vec_ref,
    ib_ref,
    wa,
    wi,
    wu,
    out_ref,
    ssg_ref,
    low_ref,
    actT_ref,
    slope_ref,
    norm_ref,
    rstd_ref,
    hidT_ref,
    sum_ref,
):
    seq, width = x_ref.shape
    blocks = wi.shape[0]
    tile = min(512, seq)
    length = len_ref[0]
    sum_ref[...] = jnp.zeros_like(sum_ref)

    def rows_step(r, carry):
        rows = aligned(r * tile, tile)
        first = x_ref[rows, :].astype(F32) + dot_nn(att_ref[rows, :], wa[3]) + vec_ref[2:3, :]
        center = first - row_mean(first)
        rstd = lax.rsqrt(row_mean(center * center) + EPSILON)
        normed = center * rstd
        norm_ref[rows, :] = normed
        rstd_ref[rows, :] = rstd
        hidden = normed * vec_ref[3:4, :] + vec_ref[4:5, :]
        low = hidden.astype(BF16)
        hidT_ref[:, rows] = low.astype(F32).T.astype(BF16)

        def block(f, second):
            inner = dot_nn(low, wi[f]) + ib_ref[pl.ds(f, 1), :]
            active, slope = gelu_parts(inner)
            active = active.astype(BF16)
            spot = aligned(f * width, width)
            slope_ref[rows, spot] = slope.astype(BF16)
            actT_ref[spot, rows] = flip(active)
            return second + dot_nn(active, wu[spot, :])

        second = lax.fori_loop(0, blocks, block, hidden + vec_ref[5:6, :], unroll=True)
        center = second - row_mean(second)
        rstd = lax.rsqrt(row_mean(center * center) + EPSILON)
        normed = center * rstd
        spot = r * tile + lax.broadcasted_iota(jnp.int32, (tile, width), 0)
        valid = spot < length
        result = normed * vec_ref[6:7, :] + vec_ref[7:8, :]
        out_ref[rows, :] = jnp.where(valid, result, 0.0).astype(BF16)
        grad = jnp.where(valid, cot_ref[rows, :].astype(F32), 0.0)
        sum_ref[7:8, :] += column_sum(grad)
        sum_ref[6:7, :] += column_sum(grad * normed)
        grad = grad * vec_ref[6:7, :]
        grad = rstd * (grad - row_mean(grad) - normed * row_mean(grad * normed))
        ssg_ref[rows, :] = grad
        low = grad.astype(BF16)
        low_ref[rows, :] = low
        sum_ref[5:6, :] += column_sum(low)
        return carry

    lax.fori_loop(0, seq // tile, rows_step, 0)


def middle_forward(length, x, att, cot, vec, ib, wa, wi, wu):
    seq, width = x.shape
    blocks = ib.shape[0]
    return pl.pallas_call(
        middle_forward_body,
        out_shape=(
            shape(seq, width),
            local(seq, width, dtype=F32),
            local(seq, width),
            local(blocks * width, seq),
            local(seq, blocks * width),
            local(seq, width, dtype=F32),
            local(seq, 1, dtype=F32),
            local(width, seq),
            local(8, width, dtype=F32),
        ),
        in_specs=[SM] + [VM] * 8,
        out_specs=[VM] * 9,
        compiler_params=limit(16),
        cost_estimate=FREE,
        name="middle_forward",
    )(length, x, *stay(att), cot, *stay(vec, ib, wa, wi, wu))


def middle_backward_body(
    low_ref, ssg_ref, slope_ref, norm_ref, rstd_ref, vec_ref, wa, wi, wu, igl_ref, fsg_ref, branch_ref, att_ref, ib_ref, sum_ref
):
    seq, width = low_ref.shape
    blocks = wi.shape[0]
    tile = min(512, seq)
    sum_ref[...] = jnp.zeros_like(sum_ref)
    ib_ref[...] = jnp.zeros_like(ib_ref)

    def rows_step(r, carry):
        rows = aligned(r * tile, tile)
        low = low_ref[rows, :]

        def block(f, grad):
            spot = aligned(f * width, width)
            inner = (dot_nt(low, wu[spot, :]) * slope_ref[rows, spot].astype(F32)).astype(BF16)
            igl_ref[f, rows, :] = inner
            ib_ref[pl.ds(f, 1), :] += column_sum(inner)
            return grad + dot_nt(inner, wi[f])

        grad = lax.fori_loop(0, blocks, block, ssg_ref[rows, :], unroll=True)
        normed = norm_ref[rows, :]
        sum_ref[4:5, :] += column_sum(grad)
        sum_ref[3:4, :] += column_sum(grad * normed)
        grad = grad * vec_ref[3:4, :]
        grad = rstd_ref[rows, :] * (grad - row_mean(grad) - normed * row_mean(grad * normed))
        fsg_ref[rows, :] = grad
        branch = grad.astype(BF16)
        branch_ref[rows, :] = branch
        sum_ref[2:3, :] += column_sum(branch)
        att_ref[rows, :] = dot_nt(branch, wa[3]).astype(BF16)
        return carry

    lax.fori_loop(0, seq // tile, rows_step, 0)


def middle_backward(low, ssg, slope, norm, rstd, vec, wa, wi, wu):
    seq, width = low.shape
    blocks = wi.shape[0]
    return pl.pallas_call(
        middle_backward_body,
        out_shape=(
            local(blocks, seq, width),
            local(seq, width, dtype=F32),
            local(seq, width),
            local(seq, width),
            local(blocks, width, dtype=F32),
            local(8, width, dtype=F32),
        ),
        in_specs=[VM] * 9,
        out_specs=[VM] * 6,
        compiler_params=limit(16),
        cost_estimate=FREE,
        name="middle_backward",
    )(*stay(low, ssg, slope, norm, rstd, vec, wa, wi, wu))


def input_grad_body(g_ref, fsg_ref, w_ref, out_ref, token_ref):
    seq, width = fsg_ref.shape
    token_ref[...] = jnp.zeros_like(token_ref)
    tile = min(512, seq)

    def rows_step(r, carry):
        rows = aligned(r * tile, tile)
        total = fsg_ref[rows, :]
        for n in range(3):
            total = total + dot_nt(g_ref[n, rows, :], w_ref[n])
        out_ref[rows, :] = total
        return carry

    lax.fori_loop(0, seq // tile, rows_step, 0)


def input_grad(g, fsg, wa):
    seq, width = fsg.shape
    return pl.pallas_call(
        input_grad_body,
        out_shape=(shape(seq, width, dtype=F32), local(8, 128, dtype=F32)),
        in_specs=[VM] * 3,
        out_specs=[VM] * 2,
        compiler_params=limit(12),
        cost_estimate=FREE,
        name="input_grad",
    )(*stay(g, fsg, wa))


Z_ORDER = (0, 2, 1, 3)


def weight_grad_body(kind, order, z_order, me_ref, left_ref, g_ref, *refs):
    sums, refs = (refs[:4], refs[4:]) if kind == "attend" else ((), refs)
    outs, left = refs[:2], refs[2]
    i, z, c = me_ref[0], me_ref[1], me_ref[2]
    part = 96
    if kind == "attend":
        extra = refs[3]
        one, two, three, ib = (r[...] for r in sums)
        row = lax.broadcasted_iota(jnp.int32, one.shape, 0)
        every = jnp.where(row < 2, three, jnp.where(row < 5, two, one))
        for f in range(8):
            extra[f] = jnp.zeros_like(extra[f])
            extra[f, :, :part] = every[:, f * part : (f + 1) * part]
            extra[f, 0:1, 128 : 128 + 4 * part] = ib[f // 2 : f // 2 + 1, f % 2 * 4 * part : (f % 2 + 1) * 4 * part]

    def block_step(spot, carry):
        block = i ^ pick(order, spot)
        for side, c_at in enumerate((1 - c, c)):
            for n, j in enumerate(z_order):
                f_at = 2 * (z ^ j) + c_at
                if kind == "outer":
                    rows = left_ref[aligned_rows(f_at * 384 + block * 96, 96), :]
                elif kind == "inner":
                    rows = left_ref[aligned_rows(f_at * 96, 96), :]
                else:
                    rows = left_ref[block // 3, aligned_rows(f_at * 96, 96), :]
                left[side * 384 + n * 96 : side * 384 + (n + 1) * 96, :] = rows
        right = g_ref[...] if kind == "outer" else g_ref[block]
        grads = dot_nn(left[...], right).reshape(2, 4, 96, 768).astype(BF16)
        for side, c_at in enumerate((1 - c, c)):
            outs[side][spot, :, :96, :] = grads[side]
            if kind == "attend":
                for n, j in enumerate(z_order):
                    outs[side][spot, n, 96:104, :] = extra[2 * (z ^ j) + c_at].astype(BF16)
        return carry

    lax.fori_loop(0, 4, block_step, 0, unroll=2)


def weight_grad(kind, order, z_order, me, left, g, sums=()):
    rows = 104 if kind == "attend" else 96
    return pl.pallas_call(
        functools.partial(weight_grad_body, kind, order, z_order),
        out_shape=(local(4, 4, rows, 768),) * 2,
        in_specs=[SM] + [VM] * (2 + len(sums)),
        out_specs=[VM] * 2,
        scratch_shapes=[pltpu.VMEM((768, left.shape[-1]), BF16)] + [pltpu.VMEM((8, 8, 768), F32)] * (kind == "attend"),
        compiler_params=limit(6),
        cost_estimate=FREE,
        name=f"weight_grad_{kind}",
    )(me, *stay(left, g, *sums))


def prepare_body(me_ref, *refs):
    vectors, weights = refs[:9], refs[9:15]
    first_ref, second_ref, pack_ref, *rows, sems = refs[15:]
    i = me_ref[0]
    part = vectors[0].shape[0]
    copies = [
        pltpu.make_async_copy(
            weights[4].at[:, pl.ds(pl.multiple_of(i * 768, 768), 768)], second_ref.at[pl.ds(0, 96), :], sems.at[0]
        ),
        pltpu.make_async_copy(weights[5].at[aligned_rows(i * 96, 96), :], second_ref.at[pl.ds(96, 96), :], sems.at[1]),
    ]
    for n in range(9):
        copies.append(pltpu.make_async_copy(vectors[n], rows[n], sems.at[3 + n]))
    for n in range(4):

        @pl.when(i == n)
        def _():
            pltpu.make_async_copy(weights[n], first_ref.at[pl.ds(0, 96), :], sems.at[2]).start()

    start_all(copies)
    pack_ref[...] = jnp.zeros_like(pack_ref)
    wait_all(copies[2:])
    for n in range(8):
        pack_ref[n : n + 1, :part] = rows[n][...].astype(F32).reshape(1, part)
    pack_ref[0:1, 128 : 128 + 4 * part] = rows[8][...].astype(F32).reshape(1, 4 * part)
    first_ref[96:104, :] = pack_ref[...].astype(BF16)
    pltpu.make_async_copy(weights[0], first_ref.at[pl.ds(0, 96), :], sems.at[2]).wait()
    wait_all(copies[:2])


def prepare(me, vectors, weights):
    return pl.pallas_call(
        prepare_body,
        out_shape=(local(104, 768), local(192, 768)),
        in_specs=[SM] + [HB] * 15,
        out_specs=[VM] * 2,
        scratch_shapes=[pltpu.VMEM((8, 768), F32)]
        + [pltpu.VMEM(v.shape, BF16) for v in vectors]
        + [pltpu.SemaphoreType.DMA((12,))],
        compiler_params=limit(2),
        cost_estimate=FREE,
        name="prepare",
    )(me, *far_off(*vectors, *weights))


def after(value, *others, cost=FREE):
    def body(*refs):
        pass

    return pl.pallas_call(
        body,
        out_shape=jax.ShapeDtypeStruct(value.shape, value.dtype),
        in_specs=[HB] * (1 + len(others)),
        out_specs=HB,
        input_output_aliases={0: 0},
        compiler_params=limit(1),
        cost_estimate=cost,
        name="after",
    )(value, *others)


def swap(value, axis, size, mask):
    return lax.ppermute(value, axis, [(n, n ^ mask) for n in range(size)])


def gather_z(piece, fsdp):
    return [swap(piece, "fsdp", fsdp, 2 * j) for j in (1, 2, 3)]


def combine(*outs, cost=FREE):
    arrays = []
    for _, parts in outs:
        for _, terms in parts:
            arrays += [a for a, _ in terms if not any(a is b for b in arrays)]

    def find(array):
        return next(n for n, b in enumerate(arrays) if b is array)

    def body(*refs):
        for out_ref, (lead, parts) in zip(refs[len(arrays) :], outs, strict=True):

            def tile(index):
                start = 0
                for rows, terms in parts:
                    found = [(find(array), at(*index)) for array, at in terms]
                    values = [refs[n][spot] for n, spot in found if spot is not None]
                    value = values[0] if len(values) == 1 else sum(v.astype(F32) for v in values).astype(BF16)
                    out_ref[(*index, slice(start, start + rows), slice(None))] = value
                    start += rows

            def step(front, last, carry):
                tile((*front, last))
                return carry

            if not lead:
                tile(())
            elif len(lead) == 1:
                lax.fori_loop(0, lead[0], functools.partial(step, ()), 0)
            else:
                for front in range(lead[0]):
                    lax.fori_loop(0, lead[1], functools.partial(step, (front,)), 0)

    return pl.pallas_call(
        body,
        out_shape=tuple(local(*lead, sum(rows for rows, _ in parts), 768) for lead, parts in outs),
        in_specs=[VM] * len(arrays),
        out_specs=[VM] * len(outs),
        compiler_params=limit(2),
        cost_estimate=cost,
        name="combine",
    )(*stay(*arrays))


def stack_three(parts):
    rows = parts[0].shape[0]

    def body(*refs):
        for n in range(3):
            refs[3][n] = refs[n][...]

    return pl.pallas_call(
        body,
        out_shape=local(3, rows, 768),
        in_specs=[VM] * 3,
        out_specs=VM,
        compiler_params=limit(2),
        cost_estimate=FREE,
        name="stack_three",
    )(*stay(*parts))


def rows_of(value, start, rows):
    (part,) = combine(((value.shape[0],), [(rows, [(value, lambda n: (n, slice(start, start + rows)))])]))
    return part


UPPER = slice(0, 48)


def held(pair, block, rows):
    return [(v, lambda b: (block, b, rows)) for v in pair]


def first_pair(pair, total):
    def out(blocks, rows, size):
        terms = []
        for n, block in enumerate(blocks):
            for array, at in held(pair, block, rows):
                terms.append((array, lambda a, b, n=n, at=at: at(b) if a == n else None))
        return (2, 4), [(size, terms)]

    return combine(out((1, 3), UPPER, 48), out((2, 3), slice(48, total), total - 48))


def second_pair(pair, over_x, over_y, total, cost=FREE):
    x = held(pair, 2, UPPER) + [(over_x, lambda b: (1, b))]
    y = held(pair, 1, slice(48, total)) + [(over_y, lambda b: (1, b))]
    return combine(((4,), [(48, x)]), ((4,), [(total - 48, y)]), cost=cost)


def last_terms(pair, overs, onwards, total, tile):
    parts = []
    for rows, size, over, onward in (
        (UPPER, 48, overs[0], onwards[0]),
        (slice(48, total), total - 48, overs[1], onwards[1]),
    ):
        terms = [(array, lambda *n, at=at: at(tile(*n))) for array, at in held(pair, 0, rows)]
        terms += [(over, lambda *n: (0, tile(*n))), (onward, lambda *n: (tile(*n),))]
        parts.append((size, terms))
    return parts


def last_pair(pair, overs, onwards, cost=FREE):
    return combine(*[((2,), last_terms(pair, overs, onwards, 96, lambda b, k=k: k + b)) for k in (0, 2)], cost=cost)


def finish(terms):
    def body(*refs):
        terms, (own_ref, small_ref) = refs[:-2], refs[-2:]
        value = sum(r[...].astype(F32) for r in terms)
        own_ref[...] = value[:96].astype(BF16)
        small_ref[...] = value[96:]

    return pl.pallas_call(
        body,
        out_shape=(local(96, 768), local(8, 768, dtype=F32)),
        in_specs=[VM] * len(terms),
        out_specs=[VM] * 2,
        compiler_params=limit(2),
        cost_estimate=FREE,
        name="finish",
    )(*stay(*terms))


def spread(value, dp):
    return (value,) + tuple(swap(value, "dp", dp, m) for m in (1, 2, 3))


def deliver_two(me, every):
    def body(me_ref, *refs):
        inner_ref, outer_ref = refs[4:]
        for away in range(4):
            block = me_ref[0] ^ away
            inner_ref[:, aligned(block * 768, 768)] = refs[away][:96, :].astype(F32)
            outer_ref[aligned(block * 96, 96), :] = refs[away][96:, :].astype(F32)

    return pl.pallas_call(
        body,
        out_shape=(shape(96, 3072, dtype=F32), shape(384, 768, dtype=F32)),
        in_specs=[SM] + [VM] * 4,
        out_specs=[VM] * 2,
        compiler_params=limit(6),
        cost_estimate=FREE,
        name="deliver_two",
    )(me, *stay(*every))


def deliver_four(me, every):
    def body(me_ref, *refs):
        outs, held_ref = refs[4:8], refs[8]
        for away in range(4):
            held_ref[me_ref[0] ^ away] = refs[away][...]
        for n in range(4):
            outs[n][...] = held_ref[n].astype(F32)

    return pl.pallas_call(
        body,
        out_shape=(shape(96, 768, dtype=F32),) * 4,
        in_specs=[SM] + [VM] * 4,
        out_specs=[VM] * 4,
        scratch_shapes=[pltpu.VMEM((4, 96, 768), BF16)],
        compiler_params=limit(4),
        cost_estimate=FREE,
        name="deliver_four",
    )(me, *stay(*every))


def pick(pieces, index):
    return jnp.where(index == 0, pieces[0], jnp.where(index == 1, pieces[1], jnp.where(index == 2, pieces[2], pieces[3])))


def on_device(
    sizes,
    tokens,
    lengths,
    cotangent,
    query_weight,
    query_bias,
    key_weight,
    value_weight,
    value_bias,
    output_weight,
    output_bias,
    first_gain,
    first_shift,
    inner_weight,
    inner_bias,
    outer_weight,
    outer_bias,
    second_gain,
    second_shift,
):
    dp, fsdp = sizes
    docs, seq, width = tokens.shape
    blocks = inner_weight.shape[1] // width
    direct = dp == 4 and fsdp == 8 and docs == 1 and query_weight.shape == (96, 768) and blocks == 4
    i = lax.axis_index("dp")
    f = lax.axis_index("fsdp")
    me = jnp.stack([i, f // 2, f % 2, jnp.zeros_like(i)]).astype(jnp.int32)

    small = (query_bias, value_bias, output_bias, first_gain, first_shift, outer_bias, second_gain, second_shift, inner_bias)
    part = query_bias.shape[0]

    if direct:
        mine = (query_weight, key_weight, value_weight, output_weight)
        piece_a, piece_m = prepare(me, small, mine + (inner_weight, outer_weight))
        z_a = gather_z(piece_a, fsdp)
        z_m = gather_z(piece_m, fsdp)
        mine_a = stack_three(z_a)
        plane_a = (swap(mine_a, "dp", dp, 1), swap(mine_a, "dp", dp, 2))
        parts_a = (rows_of(plane_a[0], 0, 48), rows_of(plane_a[1], 48, 48))
        rest_a = (swap(parts_a[0], "dp", dp, 2), swap(parts_a[1], "dp", dp, 1))
        z_m[0] = after(z_m[0], *rest_a)
        mine_m = stack_three(z_m)
        inner_m, outer_m = rows_of(mine_m, 0, 96), rows_of(mine_m, 96, 96)
        over_x = [swap(inner_m, "dp", dp, 1), None]
        over_y = [None, swap(outer_m, "dp", dp, 2)]
        over_x[1], over_y[0] = swap(outer_m, "dp", dp, 1), swap(inner_m, "dp", dp, 2)
        near_a = bundle(1, mine, ((((0, 0)),),) * 4, (after(mine_a, mine_m),) + plane_a + (piece_a,))
        far_a = (swap(near_a, "fsdp", fsdp, 1),) + tuple(swap(v, "fsdp", fsdp, 1) for v in rest_a)

        def far_at(base, row=0):
            return [[(base + n, 0, row, 96, 0)] for n in range(3)]

        group_a = Pieces(
            mine,
            (mine_a,) + plane_a + rest_a + far_a + (piece_a,),
            [(n, 0, 0) for n in range(4)],
            [(5, n) for n in range(4)],
            far_at(0) + [[(3, 0, 0, 48, 0), (4, 0, 0, 48, 48)]],
            [[(5, 4 + 3 * n, 0, 96, 0)] for n in range(3)] + [[(6, 0, 0, 48, 0), (7, 0, 0, 48, 48)]],
            True,
            (8, 0, 5),
        )
        x = tokens.reshape(seq, width)
        q, k, v, att, left_a, lse, wa, vec, ib = attend_forward(group_a, fsdp, blocks, me, lengths, after(x, mine_m))
        over_x[0], over_y[1] = after(over_x[0], att), after(over_y[1], att)
        rest_m = (swap(over_x[0], "dp", dp, 2), swap(over_y[1], "dp", dp, 1))
        spots = (tuple((0, 768 * n) for n in range(4)), tuple((96 * n, 0) for n in range(4)))

        def spots_of(n):
            return [(0, *spot) for spot in spots[n]]

        planes = ((inner_m, outer_m), over_x, over_y)
        near_m = bundle(2, (inner_weight, outer_weight), spots, tuple(v for plane in planes for v in plane))
        far_m = swap(near_m, "fsdp", fsdp, 1)
        empty = [[]]
        near_i = Pieces((inner_weight,), (inner_m, over_x[0], over_y[0]), spots_of(0), (), far_at(0) + empty, empty * 4, True)
        near_u = Pieces((outer_weight,), (outer_m, over_x[1], over_y[1]), spots_of(1), (), far_at(0) + empty, empty * 4, False)
        wi = fill(near_i, me, blocks, width, width)
        wu = fill(near_u, me, blocks * width, width)
        rest_m = [after(v, near_m, wi, wu, cost=LONG) for v in rest_m]
        far_rest = [swap(v, "fsdp", fsdp, 1) for v in rest_m]
        far_m = after(far_m, *rest_m)

        def from_sibling(first, tile, stacked):
            far = [[(0, tile + 6 * n, 0, 96, 0)] for n in range(3)] + empty
            return Pieces((), (far_m,), (), [(0, first + n) for n in range(4)], empty * 4, far, stacked)

        def late(n, stacked):
            arrays = (rest_m[n], far_rest[n])
            return Pieces((), arrays, (), (), empty * 3 + [[(0, 0, 0, 96, 0)]], empty * 3 + [[(1, 0, 0, 96, 0)]], stacked)

        wi = fill(from_sibling(0, 8, True), me, blocks, width, width, before=wi)
        wu = fill(from_sibling(4, 11, False), me, blocks * width, width, before=wu)
        far_rest[0] = after(far_rest[0], wi, wu)
        wi = fill(late(0, True), me, blocks, width, width, before=wi)
        wu = fill(late(1, False), me, blocks * width, width, before=wu)
    else:
        whole = tuple(
            lax.all_gather(w, "fsdp", axis=0, tiled=True)
            for w in (query_weight, key_weight, value_weight, output_weight, inner_weight, outer_weight)
        )
        packs = jnp.pad(jnp.stack(small[:8]), ((0, 0), (0, width - part)))
        packs = packs + jnp.pad(inner_bias[None], ((0, 7), (128, width - 128 - 4 * part)))
        packs = lax.all_gather(packs, "fsdp", axis=0, tiled=False)
        group_a = Whole(whole[:4], (packs,), [(n, 0, 0) for n in range(4)], True)
        group_i = Whole(whole[4:5], (), [(0, 0, width * n) for n in range(blocks)], True)
        group_u = Whole(whole[5:6], (), [(0, width * n, 0) for n in range(blocks)], False)
        x = tokens.reshape(seq, width)
        q, k, v, att, left_a, lse, wa, vec, ib = attend_forward(group_a, fsdp, blocks, me, lengths, x)
        wi = fill(group_i, me, blocks, width, width)
        wu = fill(group_u, me, blocks * width, width)

    cot = cotangent.reshape(seq, width)
    out, ssg, low, act_t, slope, norm, rstd, hid_t, sum_one = middle_forward(lengths, x, att, cot, vec, ib, wa, wi, wu)
    pairs = width // 128
    attend = functools.partial(attend_backward, length=lengths, q=q, k=k, v=v, lse=lse)
    if direct:
        sent_u, kept_u = weight_grad("outer", (0, 1, 2, 3), Z_ORDER, me, act_t, low)
        got_u = swap(sent_u, "fsdp", fsdp, 1)
        low = after(low, sent_u)
    igl, fsg, branch, att_g, ib_sum, sum_two = middle_backward(low, ssg, slope, norm, rstd, vec, wa, wi, wu)
    if direct:
        pair_u = (kept_u, after(got_u, igl))
        first_u = first_pair(pair_u, 96)
        over_u = [swap(first_u[0], "dp", dp, 1), swap(first_u[1], "dp", dp, 2)]
        igl = after(igl, *first_u)
        sent_i, kept_i = weight_grad("inner", (0, 1, 2, 3), Z_ORDER, me, hid_t, igl)
        got_i = swap(sent_i, "fsdp", fsdp, 1)
        third = pairs // 3
        part_one = attend(0, third, do=after(att_g, sent_i), branch=branch)
        pair_i = (kept_i, after(got_i, part_one[0]))
        first_i = first_pair(pair_i, 96)
        over_i = [swap(first_i[0], "dp", dp, 1), swap(first_i[1], "dp", dp, 2)]
        g, sum_three = attend(third, pairs, do=after(att_g, *first_i), branch=branch, before=part_one)
    else:
        g, sum_three = attend(0, pairs, do=att_g, branch=branch)
        in_grad, _ = input_grad(g, fsg, wa)

    if direct:
        here = lambda: ()
        sent_a, kept_a = weight_grad(
            "attend", (0, 1, 2, 3), (0, 1, 2, 3), me, left_a, g, (sum_one, sum_two, sum_three, ib_sum)
        )
        over_u = [after(v, kept_a) for v in over_u]
        second_u = second_pair(pair_u, *over_u, 96)
        onward_u = [swap(second_u[0], "dp", dp, 2), swap(second_u[1], "dp", dp, 1)]

        in_grad, token = input_grad(g, after(fsg, *second_u), wa)
        over_i = [after(v, token) for v in over_i]
        second_i = second_pair(pair_i, *over_i, 96, LONG)
        onward_i = [swap(second_i[0], "dp", dp, 2), swap(second_i[1], "dp", dp, 1)]

        got_a = swap(sent_a, "fsdp", fsdp, 1)
        pair_a = (kept_a, after(got_a, *second_i))
        first_a = first_pair(pair_a, 104)
        over_a = [swap(first_a[0], "dp", dp, 1), swap(first_a[1], "dp", dp, 2)]

        onward_u = [after(v, *first_a) for v in onward_u]
        keep_u, send_u = last_pair(pair_u, over_u, onward_u)
        near_u = swap(send_u, "fsdp", fsdp, 2)

        onward_i = [after(v, keep_u) for v in onward_i]
        keep_i, send_i = last_pair(pair_i, over_i, onward_i, LONG)
        near_i = swap(send_i, "fsdp", fsdp, 2)

        near_u = after(near_u, keep_i)
        (next_u,) = combine(((), [(96, [(keep_u, lambda: (1,)), (near_u, lambda: (1,))])]))
        last_u = swap(next_u, "fsdp", fsdp, 4)

        over_a = [after(v, next_u) for v in over_a]
        second_a = second_pair(pair_a, *over_a, 104)
        onward_a = [swap(second_a[0], "dp", dp, 2), swap(second_a[1], "dp", dp, 1)]

        near_i = after(near_i, *second_a)
        (next_i,) = combine(((), [(96, [(keep_i, lambda: (1,)), (near_i, lambda: (1,))])]), cost=LONG)
        last_i = swap(next_i, "fsdp", fsdp, 4)

        last_u = after(last_u, next_i)
        terms_u = [(keep_u, lambda: (0,)), (near_u, lambda: (0,)), (last_u, here)]
        (own_u,) = combine(((), [(96, terms_u)]))

        last_i = after(last_i, own_u)
        terms_i = [(keep_i, lambda: (0,)), (near_i, lambda: (0,)), (last_i, here)]
        (own_i,) = combine(((), [(96, terms_i)]))

        onward_a = [after(v, own_i) for v in onward_a]
        whole_a = combine(*[((), last_terms(pair_a, over_a, onward_a, 104, lambda j=j: j)) for j in range(4)])
        far_a = [swap(whole_a[j], "fsdp", fsdp, 2 * j) for j in (1, 2, 3)]

        (own_m,) = combine(((), [(96, [(after(own_i, whole_a[0]), here)]), (96, [(own_u, here)])]))
        every = spread(own_m, dp)

        far_a[0] = after(far_a[0], own_m)
        own_a, small_own = finish((whole_a[0], *far_a))
        all_a = spread(own_a, dp)
        small_grads = [small_own[n, :part] for n in range(8)] + [small_own[0, 128 : 128 + blocks * part]]
        i_g, u_g = deliver_two(me, every)
        q_g, k_g, v_g, o_g = deliver_four(me, all_a)
    else:
        vec_sum = jnp.concatenate([sum_three[:2], sum_two[2:5], sum_one[5:8]])
        vec_sum = vec_sum.reshape(8, fsdp, part).transpose(1, 0, 2).reshape(fsdp, 8 * part)
        ib_part = ib_sum.reshape(fsdp, blocks * part)
        small_sum = lax.psum(jnp.concatenate([vec_sum, ib_part], axis=1), ("dp", "fsdp"))
        small_own = lax.dynamic_index_in_dim(small_sum, f, 0, keepdims=False)
        small_grads = [small_own[n * part : (n + 1) * part] for n in range(8)] + [small_own[8 * part :]]
        x_t, att_t = left_a[0], left_a[1]
        locals_ = (
            dot_nn(x_t, g[0]),
            dot_nn(x_t, g[1]),
            dot_nn(x_t, g[2]),
            dot_nn(att_t, g[3]),
            jnp.concatenate([dot_nn(hid_t, igl[n]) for n in range(blocks)], axis=1),
            dot_nn(act_t, low),
        )
        owned = [lax.psum_scatter(w, "fsdp", scatter_dimension=0, tiled=True) for w in locals_]
        q_g, k_g, v_g, o_g, i_g, u_g = (lax.psum(w.astype(BF16), "dp").astype(F32) for w in owned)

    qb, vb, ob, g1, s1, ub, g2, s2, ibg = small_grads
    return (
        out.reshape(docs, seq, width),
        in_grad.reshape(docs, seq, width),
        q_g,
        qb,
        k_g,
        v_g,
        vb,
        o_g,
        ob,
        g1,
        s1,
        i_g,
        ibg,
        u_g,
        ub,
        g2,
        s2,
    )


def solution(mesh):
    rows, row = P("fsdp", None), P("fsdp")
    docs = P(("dp", "fsdp"), None, None)
    in_specs = (docs, P(("dp", "fsdp")), docs, rows, row, rows, rows, row, rows, row, row, row, rows, row, rows, row, row, row)
    out_specs = (docs, docs, rows, row, rows, rows, row, rows, row, row, row, rows, row, rows, row, row, row)
    sizes = (mesh.shape["dp"], mesh.shape["fsdp"])
    return jax.shard_map(
        functools.partial(on_device, sizes), mesh=mesh, in_specs=in_specs, out_specs=out_specs, check_vma=False
    )
```

profile of v0, /device:TPU:0, one launch (start us, length us, event | category | flops | bytes accessed | tf_op | source)
XLA Modules:
  0.0 207.2 jit_solution(14664628719490487036)
XLA Ops:
  2.5 5.1 %collective-permute-start.3 = (bf16[104,768]{1,0:T(8,128)(2,1)S(1)}, bf16[104,768]{1,0:T(8,128)(2,1)S(1)}, u32[]{:S(2)}, u32[]{:S(2)}) collective-permute-start(bf16[104,768]{1,0:T(8,128)(2,1)S(1)} %get-tuple-element.84.refs_7_.refs_12_), channel_id=1, source_target_pairs={{0,6},{1,7},{2,4},{3,5},{4,2},{5,3},{6,0},{7,1},{8,14},{9,15},{10,... | collective-permute-start | bytes 479240 | tf_op jit(solution)/shard_map/ppermute | solution.py:659
  8.2 4.4 %collective-permute-done.3.refs_2_ = bf16[104,768]{1,0:T(8,128)(2,1)S(1)} collective-permute-done((bf16[104,768]{1,0:T(8,128)(2,1)S(1)}, bf16[104,768]{1,0:T(8,128)(2,1)S(1)}, u32[]{:S(2)}, u32[]{:S(2)}) %collective-permute-start.3) | collective-permute-done | bytes 159776 | tf_op jit(solution)/shard_map/ppermute | solution.py:659
  12.6 8.5 %collective-permute-done.2.refs_1_ = bf16[104,768]{1,0:T(8,128)(2,1)S(1)} collective-permute-done((bf16[104,768]{1,0:T(8,128)(2,1)S(1)}, bf16[104,768]{1,0:T(8,128)(2,1)S(1)}, u32[]{:S(2)}, u32[]{:S(2)}) %collective-permute-start.2) | collective-permute-done | bytes 159776 | tf_op jit(solution)/shard_map/ppermute | solution.py:659
  27.7 5.5 %collective-permute-done.6.refs_0_.refs_6_ = bf16[3,104,768]{2,1,0:T(8,128)(2,1)S(1)} collective-permute-done((bf16[3,104,768]{2,1,0:T(8,128)(2,1)S(1)}, bf16[3,104,768]{2,1,0:T(8,128)(2,1)S(1)}, u32[]{:S(2)}, u32[]{:S(2)}) %collective-permute-start.6) | collective-permute-done | bytes 479264 | tf_op jit(solution)/shard_map/ppermute | solution.py:659
  41.0 10.8 %collective-permute-done.8.refs_1_ = bf16[192,768]{1,0:T(8,128)(2,1)S(1)} collective-permute-done((bf16[192,768]{1,0:T(8,128)(2,1)S(1)}, bf16[192,768]{1,0:T(8,128)(2,1)S(1)}, u32[]{:S(2)}, u32[]{:S(2)}) %collective-permute-start.8) | collective-permute-done | bytes 294944 | tf_op jit(solution)/shard_map/ppermute | solution.py:659
  58.8 10.9 %attend_forward.1 = (bf16[512,768]{1,0:T(8,128)(2,1)S(1)}, bf16[512,768]{1,0:T(8,128)(2,1)S(1)}, bf16[512,768]{1,0:T(8,128)(2,1)S(1)}, bf16[512,768]{1,0:T(8,128...) custom-call(s32[4]{0:T(128)S(1)} %pad_add_fusion.me_ref, ...), custom_call_target="tpu_custom_call" | custom-call | tf_op jit(solution)/shard_map/attend_forward/pallas_call | solution.py:256
  72.7 5.0 %collective-permute-done.16.refs_6_.refs_3_ = bf16[3,96,768]{2,1,0:T(8,128)(2,1)S(1)} collective-permute-done((bf16[3,96,768]{2,1,0:T(8,128)(2,1)S(1)}, bf16[3,96,768]{2,1,0:T(8,128)(2,1)S(1)}, u32[]{:S(2)}, u32[]{:S(2)}) %collective-permute-start.16) | collective-permute-done | bytes 442400 | tf_op jit(solution)/shard_map/ppermute | solution.py:659
  82.7 3.8 %collective-permute-done.14.refs_0_ = bf16[3,96,768]{2,1,0:T(8,128)(2,1)S(1)} collective-permute-done((bf16[3,96,768]{2,1,0:T(8,128)(2,1)S(1)}, bf16[3,96,768]{2,1,0:T(8,128)(2,1)S(1)}, u32[]{:S(2)}, u32[]{:S(2)}) %collective-permute-start.14) | collective-permute-done | bytes 442400 | tf_op jit(solution)/shard_map/ppermute | solution.py:659
  90.5 9.4 %middle_forward.1 = (bf16[512,768]{1,0:T(8,128)(2,1)}, f32[512,768]{1,0:T(8,128)S(1)}, bf16[512,768]{1,0:T(8,128)(2,1)S(1)}, bf16[3072,512]{1,0:T(8,128)(2,1)S(1...) custom-call(s32[1]{0:T(128)S(6)} %copy.117.len_ref, ...), custom_call_target="tpu_custom_call" | custom-call | tf_op jit(solution)/shard_map/middle_forward/pallas_call | solution.py:434
  100.0 3.5 %weight_grad_outer.1 = (bf16[4,4,96,768]{3,2,1,0:T(8,128)(2,1)S(1)}, bf16[4,4,96,768]{3,2,1,0:T(8,128)(2,1)S(1)}) custom-call(s32[4]{0:T(128)S(1)} %pad_add_fusion.me_ref, bf16[3072,512]{1,0:T(8,128)(2,1)S(1)} %get-tuple-element.94.left_ref, bf16[512,768]{1,0:T(8,128)(2,1)S(1)} %get-tuple-element.93.g_ref.refs_0_), custom_call_target="tpu_custom_call" | custom-call | tf_op jit(solution)/shard_map/weight_grad_outer/pallas_call | solution.py:585
  103.7 6.8 %middle_backward.1 = (bf16[4,512,768]{2,1,0:T(8,128)(2,1)S(1)}, f32[512,768]{1,0:T(8,128)S(1)}, bf16[512,768]{1,0:T(8,128)(2,1)S(1)}, bf16[512,768]{1,0:T(8,128)...) custom-call(bf16[512,768]{1,0:T(8,128)(2,1)S(1)} %after.44.low_ref, f32[512,768]{1,0:T(8,128)S(1)} %get-tuple-element.96.ssg_ref, ...), custom_call_target="tpu_custom_call" | custom-call | tf_op jit(solution)/shard_map/middle_backward/pallas_call | solution.py:494
  110.9 3.3 %weight_grad_inner.1 = (bf16[4,4,96,768]{3,2,1,0:T(8,128)(2,1)S(1)}, bf16[4,4,96,768]{3,2,1,0:T(8,128)(2,1)S(1)}) custom-call(s32[4]{0:T(128)S(1)} %pad_add_fusion.me_ref, bf16[768,512]{1,0:T(8,128)(2,1)S(1)} %get-tuple-element.101.left_ref, bf16[4,512,768]{2,1,0:T(8,128)(2,1)S(1)} %after.46.g_ref), custom_call_target="tpu_custom_call" | custom-call | tf_op jit(solution)/shard_map/weight_grad_inner/pallas_call | solution.py:585
  116.9 3.6 %attend_backward.2 = (bf16[4,512,768]{2,1,0:T(8,128)(2,1)S(1)}, f32[8,768]{1,0:T(8,128)S(1)}) custom-call(s32[1]{0:T(128)S(6)} %copy.117.len_ref, bf16[512,768]{1,0:T(8,128)(2,1)S(1)} %get-tuple-element.90.q_ref, bf16[512,768]{1,0:T(8,128)(2,1)S(1)} %get-tuple-element.91.k_ref, bf16[512,768]{1,0:T(8,128)(2,1)S(1)} %get-tuple-element.92.v_ref, ...), custom_call_target="tpu_custom_call" | custom-call | tf_op jit(solution)/shard_map/attend_backward/pallas_call | solution.py:316
  123.0 7.2 %attend_backward.3 = (bf16[4,512,768]{2,1,0:T(8,128)(2,1)S(1)}, f32[8,768]{1,0:T(8,128)S(1)}) custom-call(s32[1]{0:T(128)S(6)} %copy.117.len_ref, bf16[512,768]{1,0:T(8,128)(2,1)S(1)} %get-tuple-element.90.q_ref, bf16[512,768]{1,0:T(8,128)(2,1)S(1)} %get-tuple-element.91.k_ref, ...), custom_call_target="tpu_custom_call", output_to_operand_aliasing={{0}: (7, {}), {1}: (8, {})} | custom-call | tf_op jit(solution)/shard_map/attend_backward/pallas_call | solution.py:316
  130.1 3.4 %weight_grad_attend.1 = (bf16[4,4,104,768]{3,2,1,0:T(8,128)(2,1)S(1)}, bf16[4,4,104,768]{3,2,1,0:T(8,128)(2,1)S(1)}) custom-call(s32[4]{0:T(128)S(1)} %pad_add_fusion.me_ref, bf16[2,768,512]{2,1,0:T(8,128)(2,1)S(1)} %get-tuple-element.116.left_ref, bf16[4,512,768]{2,1,0:T(8,128)(2,1)S(1)} %get-tuple-element.114.g_ref, ...), custom_call_target="tpu_custom_call" | custom-call | tf_op jit(solution)/shard_map/weight_grad_attend/pallas_call | solution.py:585
  135.9 3.2 %input_grad.1 = (f32[512,768]{1,0:T(8,128)}, f32[8,128]{1,0:T(8,128)S(1)}) custom-call(bf16[4,512,768]{2,1,0:T(8,128)(2,1)S(1)} %get-tuple-element.114.g_ref, f32[512,768]{1,0:T(8,128)S(1)} %after.52.fsg_ref, bf16[4,768,768]{2,1,0:T(8,128)(2,1)S(1)} %get-tuple-element.88.wa.w_ref), custom_call_target="tpu_custom_call" | custom-call | tf_op jit(solution)/shard_map/input_grad/pallas_call | solution.py:530
  139.1 4.5 %collective-permute-done.28.refs_0_ = bf16[2,4,48,768]{3,2,1,0:T(8,128)(2,1)S(1)} collective-permute-done((bf16[2,4,48,768]{3,2,1,0:T(8,128)(2,1)S(1)}, bf16[2,4,48,768]{3,2,1,0:T(8,128)(2,1)S(1)}, u32[]{:S(2)}, u32[]{:S(2)}) %collective-permute-start.28) | collective-permute-done | bytes 589856 | tf_op jit(solution)/shard_map/ppermute | solution.py:659
  152.5 4.4 %collective-permute-done.34.refs_0_ = bf16[4,48,768]{2,1,0:T(8,128)(2,1)S(1)} collective-permute-done((bf16[4,48,768]{2,1,0:T(8,128)(2,1)S(1)}, bf16[4,48,768]{2,1,0:T(8,128)(2,1)S(1)}, u32[]{:S(2)}, u32[]{:S(2)}) %collective-permute-start.34) | collective-permute-done | bytes 294944 | tf_op jit(solution)/shard_map/ppermute | solution.py:659
  157.3 5.0 %collective-permute-done.32.refs_0_ = bf16[2,96,768]{2,1,0:T(8,128)(2,1)S(1)} collective-permute-done((bf16[2,96,768]{2,1,0:T(8,128)(2,1)S(1)}, bf16[2,96,768]{2,1,0:T(8,128)(2,1)S(1)}, u32[]{:S(2)}, u32[]{:S(2)}) %collective-permute-start.32) | collective-permute-done | bytes 294944 | tf_op jit(solution)/shard_map/ppermute | solution.py:659
  162.7 5.6 %collective-permute-done.29.refs_0_ = bf16[2,4,48,768]{3,2,1,0:T(8,128)(2,1)S(1)} collective-permute-done((bf16[2,4,48,768]{3,2,1,0:T(8,128)(2,1)S(1)}, bf16[2,4,48,768]{3,2,1,0:T(8,128)(2,1)S(1)}, u32[]{:S(2)}, u32[]{:S(2)}) %collective-permute-start.29) | collective-permute-done | bytes 589856 | tf_op jit(solution)/shard_map/ppermute | solution.py:659
  172.7 8.1 %collective-permute-done.38.refs_0_ = bf16[96,768]{1,0:T(8,128)(2,1)S(1)} collective-permute-done((bf16[96,768]{1,0:T(8,128)(2,1)S(1)}, bf16[96,768]{1,0:T(8,128)(2,1)S(1)}, u32[]{:S(2)}, u32[]{:S(2)}) %collective-permute-start.38) | collective-permute-done | bytes 147488 | tf_op jit(solution)/shard_map/ppermute | solution.py:659
  182.8 2.8 %collective-permute-start.42 = (bf16[104,768]{1,0:T(8,128)(2,1)S(1)}, bf16[104,768]{1,0:T(8,128)(2,1)S(1)}, u32[]{:S(2)}, u32[]{:S(2)}) collective-permute-start(bf16[104,768]{1,0:T(8,128)(2,1)S(1)} %get-tuple-element.139), channel_id=1, source_target_pairs={{0,4},{1,5},{2,6},{3,7},{4,0},{5,1},{6,2},{7,3},{8,12},{9,13},{10,... | collective-permute-start | bytes 479240 | tf_op jit(solution)/shard_map/ppermute | solution.py:659
  187.7 3.0 %collective-permute-done.41.refs_0_ = bf16[104,768]{1,0:T(8,128)(2,1)S(1)} collective-permute-done((bf16[104,768]{1,0:T(8,128)(2,1)S(1)}, bf16[104,768]{1,0:T(8,128)(2,1)S(1)}, u32[]{:S(2)}, u32[]{:S(2)}) %collective-permute-start.41) | collective-permute-done | bytes 159776 | tf_op jit(solution)/shard_map/ppermute | solution.py:659
  191.9 5.5 %collective-permute-done.42.refs_2_ = bf16[104,768]{1,0:T(8,128)(2,1)S(1)} collective-permute-done((bf16[104,768]{1,0:T(8,128)(2,1)S(1)}, bf16[104,768]{1,0:T(8,128)(2,1)S(1)}, u32[]{:S(2)}, u32[]{:S(2)}) %collective-permute-start.42) | collective-permute-done | bytes 159776 | tf_op jit(solution)/shard_map/ppermute | solution.py:659
  (164 shorter events, 71.7 us)
Async XLA Ops:
  7.6 13.5 %collective-permute-start.2 = (bf16[104,768]{1,0:T(8,128)(2,1)S(1)}, bf16[104,768]{1,0:T(8,128)(2,1)S(1)}, u32[]{:S(2)}, u32[]{:S(2)}) collective-permute-start(bf16[104,768]{1,0:T(8,128)(2,1)S(1)} %get-tuple-element.84.refs_7_.refs_12_), channel_id=1, source_target_pairs={{0,4},{1,5},{2,6},{3,7},{4,0},{5,1},{6,2},{7,3},{8,12},{9,13},{10,... | collective-permute-start | bytes 479240 | tf_op jit(solution)/shard_map/ppermute | solution.py:659
  7.6 13.5 %collective-permute-start.1 = (bf16[104,768]{1,0:T(8,128)(2,1)S(1)}, bf16[104,768]{1,0:T(8,128)(2,1)S(1)}, u32[]{:S(2)}, u32[]{:S(2)}) collective-permute-start(bf16[104,768]{1,0:T(8,128)(2,1)S(1)} %get-tuple-element.84.refs_7_.refs_12_), channel_id=1, source_target_pairs={{0,2},{1,3},{2,0},{3,1},{4,6},{5,7},{6,4},{7,5},{8,10},{9,11},{10,... | collective-permute-start | bytes 479240 | tf_op jit(solution)/shard_map/ppermute | solution.py:659
  24.2 13.0 %collective-permute-start = (bf16[192,768]{1,0:T(8,128)(2,1)S(1)}, bf16[192,768]{1,0:T(8,128)(2,1)S(1)}, u32[]{:S(2)}, u32[]{:S(2)}) collective-permute-start(bf16[192,768]{1,0:T(8,128)(2,1)S(1)} %get-tuple-element.83), channel_id=1, source_target_pairs={{0,2},{1,3},{2,0},{3,1},{4,6},{5,7},{6,4},{7,5},{8,10},{9,11},{10,... | collective-permute-start | bytes 884744 | tf_op jit(solution)/shard_map/ppermute | solution.py:659
  24.2 16.8 %collective-permute-start.9 = (bf16[192,768]{1,0:T(8,128)(2,1)S(1)}, bf16[192,768]{1,0:T(8,128)(2,1)S(1)}, u32[]{:S(2)}, u32[]{:S(2)}) collective-permute-start(bf16[192,768]{1,0:T(8,128)(2,1)S(1)} %get-tuple-element.83), channel_id=1, source_target_pairs={{0,6},{1,7},{2,4},{3,5},{4,2},{5,3},{6,0},{7,1},{8,14},{9,15},{10,... | collective-permute-start | bytes 884744 | tf_op jit(solution)/shard_map/ppermute | solution.py:659
  26.7 25.2 %collective-permute-start.8 = (bf16[192,768]{1,0:T(8,128)(2,1)S(1)}, bf16[192,768]{1,0:T(8,128)(2,1)S(1)}, u32[]{:S(2)}, u32[]{:S(2)}) collective-permute-start(bf16[192,768]{1,0:T(8,128)(2,1)S(1)} %get-tuple-element.83), channel_id=1, source_target_pairs={{0,4},{1,5},{2,6},{3,7},{4,0},{5,1},{6,2},{7,3},{8,12},{9,13},{10,... | collective-permute-start | bytes 884744 | tf_op jit(solution)/shard_map/ppermute | solution.py:659
  53.3 16.3 %collective-permute-start.13 = (bf16[3,96,768]{2,1,0:T(8,128)(2,1)S(1)}, bf16[3,96,768]{2,1,0:T(8,128)(2,1)S(1)}, u32[]{:S(2)}, u32[]{:S(2)}) collective-permute-start(bf16[3,96,768]{2,1,0:T(8,128)(2,1)S(1)} %combine.20.refs_2_.refs_1_), channel_id=1, source_target_pairs={{0,8},{8,0},{16,24},{24,16},{1,9},{9,1},{17,25},{25,17},{2,10},{10... | collective-permute-start | bytes 1327112 | tf_op jit(solution)/shard_map/ppermute | solution.py:659
  55.2 16.0 %collective-permute-start.17 = (bf16[3,96,768]{2,1,0:T(8,128)(2,1)S(1)}, bf16[3,96,768]{2,1,0:T(8,128)(2,1)S(1)}, u32[]{:S(2)}, u32[]{:S(2)}) collective-permute-start(bf16[3,96,768]{2,1,0:T(8,128)(2,1)S(1)} %combine.21.refs_3_.refs_1_), channel_id=1, source_target_pairs={{0,16},{8,24},{16,0},{24,8},{1,17},{9,25},{17,1},{25,9},{2,18},{10... | collective-permute-start | bytes 1327112 | tf_op jit(solution)/shard_map/ppermute | solution.py:659
  57.7 20.1 %collective-permute-start.16 = (bf16[3,96,768]{2,1,0:T(8,128)(2,1)S(1)}, bf16[3,96,768]{2,1,0:T(8,128)(2,1)S(1)}, u32[]{:S(2)}, u32[]{:S(2)}) collective-permute-start(bf16[3,96,768]{2,1,0:T(8,128)(2,1)S(1)} %combine.20.refs_2_.refs_1_), channel_id=1, source_target_pairs={{0,16},{8,24},{16,0},{24,8},{1,17},{9,25},{17,1},{25,9},{2,18},{10... | collective-permute-start | bytes 1327112 | tf_op jit(solution)/shard_map/ppermute | solution.py:659
  58.2 19.5 %collective-permute-start.15 = (bf16[3,96,768]{2,1,0:T(8,128)(2,1)S(1)}, bf16[3,96,768]{2,1,0:T(8,128)(2,1)S(1)}, u32[]{:S(2)}, u32[]{:S(2)}) collective-permute-start(bf16[3,96,768]{2,1,0:T(8,128)(2,1)S(1)} %combine.21.refs_3_.refs_1_), channel_id=1, source_target_pairs={{0,8},{8,0},{16,24},{24,16},{1,9},{9,1},{17,25},{25,17},{2,10},{10... | collective-permute-start | bytes 1327112 | tf_op jit(solution)/shard_map/ppermute | solution.py:659
  69.7 16.8 %collective-permute-start.14 = (bf16[3,96,768]{2,1,0:T(8,128)(2,1)S(1)}, bf16[3,96,768]{2,1,0:T(8,128)(2,1)S(1)}, u32[]{:S(2)}, u32[]{:S(2)}) collective-permute-start(bf16[3,96,768]{2,1,0:T(8,128)(2,1)S(1)} %after.38.refs_4_.refs_2_), channel_id=1, source_target_pairs={{0,16},{8,24},{16,0},{24,8},{1,17},{9,25},{17,1},{25,9},{2,18},{10... | collective-permute-start | bytes 1327112 | tf_op jit(solution)/shard_map/ppermute | solution.py:659
  71.2 15.3 %collective-permute-start.20 = (bf16[3,96,768]{2,1,0:T(8,128)(2,1)S(1)}, bf16[3,96,768]{2,1,0:T(8,128)(2,1)S(1)}, u32[]{:S(2)}, u32[]{:S(2)}) collective-permute-start(bf16[3,96,768]{2,1,0:T(8,128)(2,1)S(1)} %after.39.refs_7_.refs_3_), channel_id=1, source_target_pairs={{0,8},{8,0},{16,24},{24,16},{1,9},{9,1},{17,25},{25,17},{2,10},{10... | collective-permute-start | bytes 1327112 | tf_op jit(solution)/shard_map/ppermute | solution.py:659
  114.8 18.8 %collective-permute-start.25 = (bf16[2,4,48,768]{3,2,1,0:T(8,128)(2,1)S(1)}, bf16[2,4,48,768]{3,2,1,0:T(8,128)(2,1)S(1)}, u32[]{:S(2)}, u32[]{:S(2)}) collective-permute-start(bf16[2,4,48,768]{3,2,1,0:T(8,128)(2,1)S(1)} %get-tuple-element.105.refs_2_), channel_id=1, source_target_pairs={{0,16},{8,24},{16,0},{24,8},{1,17},{9,25},{17,1},{25,9},{2,18},{10... | collective-permute-start | bytes 1769480 | tf_op jit(solution)/shard_map/ppermute | solution.py:659
  115.4 18.2 %collective-permute-start.24 = (bf16[2,4,48,768]{3,2,1,0:T(8,128)(2,1)S(1)}, bf16[2,4,48,768]{3,2,1,0:T(8,128)(2,1)S(1)}, u32[]{:S(2)}, u32[]{:S(2)}) collective-permute-start(bf16[2,4,48,768]{3,2,1,0:T(8,128)(2,1)S(1)} %get-tuple-element.104.refs_1_), channel_id=1, source_target_pairs={{0,8},{8,0},{16,24},{24,16},{1,9},{9,1},{17,25},{25,17},{2,10},{10... | collective-permute-start | bytes 1769480 | tf_op jit(solution)/shard_map/ppermute | solution.py:659
  120.8 22.9 %collective-permute-start.28 = (bf16[2,4,48,768]{3,2,1,0:T(8,128)(2,1)S(1)}, bf16[2,4,48,768]{3,2,1,0:T(8,128)(2,1)S(1)}, u32[]{:S(2)}, u32[]{:S(2)}) collective-permute-start(bf16[2,4,48,768]{3,2,1,0:T(8,128)(2,1)S(1)} %get-tuple-element.112.refs_2_), channel_id=1, source_target_pairs={{0,16},{8,24},{16,0},{24,8},{1,17},{9,25},{17,1},{25,9},{2,18},{10... | collective-permute-start | bytes 1769480 | tf_op jit(solution)/shard_map/ppermute | solution.py:659
  122.4 21.8 %collective-permute-start.27 = (bf16[2,4,48,768]{3,2,1,0:T(8,128)(2,1)S(1)}, bf16[2,4,48,768]{3,2,1,0:T(8,128)(2,1)S(1)}, u32[]{:S(2)}, u32[]{:S(2)}) collective-permute-start(bf16[2,4,48,768]{3,2,1,0:T(8,128)(2,1)S(1)} %get-tuple-element.111.refs_1_), channel_id=1, source_target_pairs={{0,8},{8,0},{16,24},{24,16},{1,9},{9,1},{17,25},{25,17},{2,10},{10... | collective-permute-start | bytes 1769480 | tf_op jit(solution)/shard_map/ppermute | solution.py:659
  133.9 18.2 %collective-permute-start.30 = (bf16[4,48,768]{2,1,0:T(8,128)(2,1)S(1)}, bf16[4,48,768]{2,1,0:T(8,128)(2,1)S(1)}, u32[]{:S(2)}, u32[]{:S(2)}) collective-permute-start(bf16[4,48,768]{2,1,0:T(8,128)(2,1)S(1)} %get-tuple-element.122.refs_1_), channel_id=1, source_target_pairs={{0,16},{8,24},{16,0},{24,8},{1,17},{9,25},{17,1},{25,9},{2,18},{10... | collective-permute-start | bytes 884744 | tf_op jit(solution)/shard_map/ppermute | solution.py:659
  134.4 16.1 %collective-permute-start.31 = (bf16[4,48,768]{2,1,0:T(8,128)(2,1)S(1)}, bf16[4,48,768]{2,1,0:T(8,128)(2,1)S(1)}, u32[]{:S(2)}, u32[]{:S(2)}) collective-permute-start(bf16[4,48,768]{2,1,0:T(8,128)(2,1)S(1)} %get-tuple-element.123.refs_2_), channel_id=1, source_target_pairs={{0,8},{8,0},{16,24},{24,16},{1,9},{9,1},{17,25},{25,17},{2,10},{10... | collective-permute-start | bytes 884744 | tf_op jit(solution)/shard_map/ppermute | solution.py:659
  144.5 12.4 %collective-permute-start.34 = (bf16[4,48,768]{2,1,0:T(8,128)(2,1)S(1)}, bf16[4,48,768]{2,1,0:T(8,128)(2,1)S(1)}, u32[]{:S(2)}, u32[]{:S(2)}) collective-permute-start(bf16[4,48,768]{2,1,0:T(8,128)(2,1)S(1)} %get-tuple-element.128.refs_2_), channel_id=1, source_target_pairs={{0,8},{8,0},{16,24},{24,16},{1,9},{9,1},{17,25},{25,17},{2,10},{10... | collective-permute-start | bytes 884744 | tf_op jit(solution)/shard_map/ppermute | solution.py:659
  147.9 20.4 %collective-permute-start.29 = (bf16[2,4,48,768]{3,2,1,0:T(8,128)(2,1)S(1)}, bf16[2,4,48,768]{3,2,1,0:T(8,128)(2,1)S(1)}, u32[]{:S(2)}, u32[]{:S(2)}) collective-permute-start(bf16[2,4,48,768]{3,2,1,0:T(8,128)(2,1)S(1)} %get-tuple-element.129.refs_1_), channel_id=1, source_target_pairs={{0,8},{8,0},{16,24},{24,16},{1,9},{9,1},{17,25},{25,17},{2,10},{10... | collective-permute-start | bytes 1769480 | tf_op jit(solution)/shard_map/ppermute | solution.py:659
  150.5 19.6 %collective-permute-start.35 = (bf16[2,4,56,768]{3,2,1,0:T(8,128)(2,1)S(1)}, bf16[2,4,56,768]{3,2,1,0:T(8,128)(2,1)S(1)}, u32[]{:S(2)}, u32[]{:S(2)}) collective-permute-start(bf16[2,4,56,768]{3,2,1,0:T(8,128)(2,1)S(1)} %get-tuple-element.130.refs_2_), channel_id=1, source_target_pairs={{0,16},{8,24},{16,0},{24,8},{1,17},{9,25},{17,1},{25,9},{2,18},{10... | collective-permute-start | bytes 2064392 | tf_op jit(solution)/shard_map/ppermute | solution.py:659
  157.2 15.3 %collective-permute-start.37 = (bf16[2,96,768]{2,1,0:T(8,128)(2,1)S(1)}, bf16[2,96,768]{2,1,0:T(8,128)(2,1)S(1)}, u32[]{:S(2)}, u32[]{:S(2)}) collective-permute-start(bf16[2,96,768]{2,1,0:T(8,128)(2,1)S(1)} %get-tuple-element.135), channel_id=1, source_target_pairs={{0,2},{1,3},{2,0},{3,1},{4,6},{5,7},{6,4},{7,5},{8,10},{9,11},{10,... | collective-permute-start | bytes 884744 | tf_op jit(solution)/shard_map/ppermute | solution.py:659
  181.2 19.2 %collective-permute-start.49 = (bf16[192,768]{1,0:T(8,128)(2,1)S(1)}, bf16[192,768]{1,0:T(8,128)(2,1)S(1)}, u32[]{:S(2)}, u32[]{:S(2)}) collective-permute-start(bf16[192,768]{1,0:T(8,128)(2,1)S(1)} %combine.35.refs_1_.refs_0_), channel_id=1, source_target_pairs={{0,24},{8,16},{16,8},{24,0},{1,25},{9,17},{17,9},{25,1},{2,26},{10... | collective-permute-start | bytes 884744 | tf_op jit(solution)/shard_map/ppermute | solution.py:659
  182.8 14.6 %collective-permute-start.42 = (bf16[104,768]{1,0:T(8,128)(2,1)S(1)}, bf16[104,768]{1,0:T(8,128)(2,1)S(1)}, u32[]{:S(2)}, u32[]{:S(2)}) collective-permute-start(bf16[104,768]{1,0:T(8,128)(2,1)S(1)} %get-tuple-element.139), channel_id=1, source_target_pairs={{0,4},{1,5},{2,6},{3,7},{4,0},{5,1},{6,2},{7,3},{8,12},{9,13},{10,... | collective-permute-start | bytes 479240 | tf_op jit(solution)/shard_map/ppermute | solution.py:659
  187.2 15.0 %collective-permute-start.48 = (bf16[192,768]{1,0:T(8,128)(2,1)S(1)}, bf16[192,768]{1,0:T(8,128)(2,1)S(1)}, u32[]{:S(2)}, u32[]{:S(2)}) collective-permute-start(bf16[192,768]{1,0:T(8,128)(2,1)S(1)} %combine.35.refs_1_.refs_0_), channel_id=1, source_target_pairs={{0,16},{8,24},{16,0},{24,8},{1,17},{9,25},{17,1},{25,9},{2,18},{10... | collective-permute-start | bytes 884744 | tf_op jit(solution)/shard_map/ppermute | solution.py:659
  (29 other events, 208.2 us)
where the time goes:
time: 208 us; the launch traced here: 207 us
  waiting for transfers between devices  86.6 us (42%)
  Pallas kernels  69.1 us (33%)
  starting transfers between devices  47.8 us (23%)
    ppermute x50, waiting for transfers between devices, swap(): return lax.ppermute(value, axis, [(n, n ^ mask) for n in range(size)])  86.6 us
    ppermute x50, starting transfers between devices, swap(): return lax.ppermute(value, axis, [(n, n ^ mask) for n in range(size)])  47.8 us
    pallas_call x1, Pallas kernels, attend_forward(): pl.pallas_call(functools.partial(attend_forward_body, group, width // sha...  10.9 us
    pallas_call x2, Pallas kernels, attend_backward(): pl.pallas_call(functools.partial(attend_backward_body, first, last), out_...  10.8 us
    pallas_call x3, Pallas kernels, weight_grad(): pl.pallas_call(functools.partial(weight_grad_body, kind, order, z_order),...  10.3 us
    pallas_call x1, Pallas kernels, middle_forward(): pl.pallas_call(middle_forward_body, out_shape=(shape(seq, width), local(s...  9.45 us
    pallas_call x1, Pallas kernels, middle_backward(): pl.pallas_call(middle_backward_body, out_shape=(local(blocks, seq, width)...  6.84 us
    pallas_call x6, Pallas kernels, fill(): pl.pallas_call(functools.partial(fill_body, group, early), out_shape=loca...  6.33 us
  transfers between devices with their start and end apart: 50, of which 23 were waited for; matrix products, arithmetic and copies ran while one was open for 1% of the time, Pallas kernels for 22%

commit v1 on v0

--- a/solution.py
+++ b/solution.py
@@ -659,10 +659,6 @@
     return lax.ppermute(value, axis, [(n, n ^ mask) for n in range(size)])
 
 
-def gather_z(piece, fsdp):
-    return [swap(piece, "fsdp", fsdp, 2 * j) for j in (1, 2, 3)]
-
-
 def combine(*outs, cost=FREE):
     arrays = []
     for _, parts in outs:
@@ -707,22 +703,26 @@
     )(*stay(*arrays))
 
 
-def stack_three(parts):
-    rows = parts[0].shape[0]
-
+def stack(rows, *tiles, cost=FREE):
     def body(*refs):
-        for n in range(3):
-            refs[3][n] = refs[n][...]
+        for n, (_, place, first) in enumerate(tiles):
+            part = pl.ds(first, rows)
+            refs[-1][n] = refs[n][part, :] if place is None else refs[n][place, part, :]
 
     return pl.pallas_call(
         body,
-        out_shape=local(3, rows, 768),
-        in_specs=[VM] * 3,
+        out_shape=local(len(tiles), rows, 768),
+        in_specs=[VM] * len(tiles),
         out_specs=VM,
         compiler_params=limit(2),
-        cost_estimate=FREE,
-        name="stack_three",
-    )(*stay(*parts))
+        cost_estimate=cost,
+        name="stack",
+    )(*stay(*(array for array, _, _ in tiles)))
+
+
+def pair_up(piece, fsdp, cost=FREE):
+    other = swap(piece, "fsdp", fsdp, 4)
+    return other, lambda ready: stack(piece.shape[0], (piece, None, 0), (ready, None, 0), cost=cost)
 
 
 def rows_of(value, start, rows):
@@ -870,19 +870,23 @@
     if direct:
         mine = (query_weight, key_weight, value_weight, output_weight)
         piece_a, piece_m = prepare(me, small, mine + (inner_weight, outer_weight))
-        z_a = gather_z(piece_a, fsdp)
-        z_m = gather_z(piece_m, fsdp)
-        mine_a = stack_three(z_a)
+        other_a, with_a = pair_up(piece_a, fsdp)
+        other_m, with_m = pair_up(piece_m, fsdp, LONG)
+        pair_a = with_a(other_a)
+        beside_a = swap(pair_a, "fsdp", fsdp, 2)
+        mine_a = stack(104, (beside_a, 0, 0), (other_a, None, 0), (beside_a, 1, 0))
+        other_m = after(other_m, mine_a)
+        beside_m = swap(with_m(other_m), "fsdp", fsdp, 2)
         plane_a = (swap(mine_a, "dp", dp, 1), swap(mine_a, "dp", dp, 2))
+        plane_a = tuple(after(v, other_m) for v in plane_a)
         parts_a = (rows_of(plane_a[0], 0, 48), rows_of(plane_a[1], 48, 48))
         rest_a = (swap(parts_a[0], "dp", dp, 2), swap(parts_a[1], "dp", dp, 1))
-        z_m[0] = after(z_m[0], *rest_a)
-        mine_m = stack_three(z_m)
-        inner_m, outer_m = rows_of(mine_m, 0, 96), rows_of(mine_m, 96, 96)
+        beside_m = after(beside_m, *rest_a)
+        inner_m, outer_m = (stack(96, (beside_m, 0, n), (other_m, None, n), (beside_m, 1, n)) for n in (0, 96))
         over_x = [swap(inner_m, "dp", dp, 1), None]
         over_y = [None, swap(outer_m, "dp", dp, 2)]
         over_x[1], over_y[0] = swap(outer_m, "dp", dp, 1), swap(inner_m, "dp", dp, 2)
-        near_a = bundle(1, mine, ((((0, 0)),),) * 4, (after(mine_a, mine_m),) + plane_a + (piece_a,))
+        near_a = bundle(1, mine, ((((0, 0)),),) * 4, (after(mine_a, inner_m),) + plane_a + (piece_a,))
         far_a = (swap(near_a, "fsdp", fsdp, 1),) + tuple(swap(v, "fsdp", fsdp, 1) for v in rest_a)
 
         def far_at(base, row=0):
@@ -899,7 +903,7 @@
             (8, 0, 5),
         )
         x = tokens.reshape(seq, width)
-        q, k, v, att, left_a, lse, wa, vec, ib = attend_forward(group_a, fsdp, blocks, me, lengths, after(x, mine_m))
+        q, k, v, att, left_a, lse, wa, vec, ib = attend_forward(group_a, fsdp, blocks, me, lengths, after(x, inner_m))
         over_x[0], over_y[1] = after(over_x[0], att), after(over_y[1], att)
         rest_m = (swap(over_x[0], "dp", dp, 2), swap(over_y[1], "dp", dp, 1))
         spots = (tuple((0, 768 * n) for n in range(4)), tuple((96 * n, 0) for n in range(4)))

time: 208 us -> 205 us (0.986)
  waiting for transfers between devices: 86.6 us -> 81.9 us
  starting transfers between devices: 47.8 us -> 49.9 us
    ppermute x50 -> x48, waiting for transfers between devices: 86.6 us -> 81.9 us  [swap(): return lax.ppermute(value, axis, [(n, n ^ mask) for n in range(size)])]
    ppermute x50 -> x48, starting transfers between devices: 47.8 us -> 49.9 us  [swap(): return lax.ppermute(value, axis, [(n, n ^ mask) for n in range(size)])]
  transfers between devices with their start and end apart: 50 -> 48, of which waited for: 23 -> 22; matrix products, arithmetic and copies ran while one was open for 1% -> 1% of each run, Pallas kernels for 22% -> 23%
where the time goes in v1:
time: 205 us
  waiting for transfers between devices  81.9 us (40%)
  Pallas kernels  69.1 us (34%)
  starting transfers between devices  49.9 us (24%)
    ppermute x48, waiting for transfers between devices, swap(): return lax.ppermute(value, axis, [(n, n ^ mask) for n in range(size)])  81.9 us
    ppermute x48, starting transfers between devices, swap(): return lax.ppermute(value, axis, [(n, n ^ mask) for n in range(size)])  49.9 us
    pallas_call x1, Pallas kernels, attend_forward(): pl.pallas_call(functools.partial(attend_forward_body, group, width // sha...  10.9 us
    pallas_call x2, Pallas kernels, attend_backward(): pl.pallas_call(functools.partial(attend_backward_body, first, last), out_...  10.7 us
    pallas_call x3, Pallas kernels, weight_grad(): pl.pallas_call(functools.partial(weight_grad_body, kind, order, z_order),...  10.3 us
    pallas_call x1, Pallas kernels, middle_forward(): pl.pallas_call(middle_forward_body, out_shape=(shape(seq, width), local(s...  9.45 us
    pallas_call x1, Pallas kernels, middle_backward(): pl.pallas_call(middle_backward_body, out_shape=(local(blocks, seq, width)...  6.87 us
    pallas_call x6, Pallas kernels, fill(): pl.pallas_call(functools.partial(fill_body, group, early), out_shape=loca...  6.33 us
  transfers between devices with their start and end apart: 48, of which 22 were waited for; matrix products, arithmetic and copies ran while one was open for 1% of the time, Pallas kernels for 23%

profile of v1, /device:TPU:0, one launch (start us, length us, event | category | flops | bytes accessed | tf_op | source)
XLA Modules:
  0.0 204.6 jit_solution(6548070032917424694)
XLA Ops:
  2.5 4.1 %collective-permute-start.1 = (bf16[104,768]{1,0:T(8,128)(2,1)S(1)}, bf16[104,768]{1,0:T(8,128)(2,1)S(1)}, u32[]{:S(2)}, u32[]{:S(2)}) collective-permute-start(bf16[104,768]{1,0:T(8,128)(2,1)S(1)} %get-tuple-element.84.refs_0_.refs_7_.refs_12_), channel_id=1, source_target_pairs={{0,4},{1,5},{2,6},{3,7},{4,0},{5,1},{6,2},{7,3},{8,12},{9,13},{10,... | collective-permute-start | bytes 479240 | tf_op jit(solution)/shard_map/ppermute | solution.py:659
  6.6 7.5 %collective-permute-done.1.refs_1_ = bf16[104,768]{1,0:T(8,128)(2,1)S(1)} collective-permute-done((bf16[104,768]{1,0:T(8,128)(2,1)S(1)}, bf16[104,768]{1,0:T(8,128)(2,1)S(1)}, u32[]{:S(2)}, u32[]{:S(2)}) %collective-permute-start.1) | collective-permute-done | bytes 159776 | tf_op jit(solution)/shard_map/ppermute | solution.py:659
  14.9 3.4 %collective-permute-start = (bf16[192,768]{1,0:T(8,128)(2,1)S(1)}, bf16[192,768]{1,0:T(8,128)(2,1)S(1)}, u32[]{:S(2)}, u32[]{:S(2)}) collective-permute-start(bf16[192,768]{1,0:T(8,128)(2,1)S(1)} %get-tuple-element.83.refs_0_), channel_id=1, source_target_pairs={{0,4},{1,5},{2,6},{3,7},{4,0},{5,1},{6,2},{7,3},{8,12},{9,13},{10,... | collective-permute-start | bytes 884744 | tf_op jit(solution)/shard_map/ppermute | solution.py:659
  18.3 10.9 %collective-permute-done.2.refs_0_.refs_2_ = bf16[2,104,768]{2,1,0:T(8,128)(2,1)S(1)} collective-permute-done((bf16[2,104,768]{2,1,0:T(8,128)(2,1)S(1)}, bf16[2,104,768]{2,1,0:T(8,128)(2,1)S(1)}, u32[]{:S(2)}, u32[]{:S(2)}) %collective-permute-start.2) | collective-permute-done | bytes 319520 | tf_op jit(solution)/shard_map/ppermute | solution.py:659
  32.4 8.1 %collective-permute-done.6.refs_0_ = bf16[3,104,768]{2,1,0:T(8,128)(2,1)S(1)} collective-permute-done((bf16[3,104,768]{2,1,0:T(8,128)(2,1)S(1)}, bf16[3,104,768]{2,1,0:T(8,128)(2,1)S(1)}, u32[]{:S(2)}, u32[]{:S(2)}) %collective-permute-start.6) | collective-permute-done | bytes 479264 | tf_op jit(solution)/shard_map/ppermute | solution.py:659
  55.9 10.9 %attend_forward.1 = (bf16[512,768]{1,0:T(8,128)(2,1)S(1)}, bf16[512,768]{1,0:T(8,128)(2,1)S(1)}, bf16[512,768]{1,0:T(8,128)(2,1)S(1)}, bf16[512,768]{1,0:T(8,128...) custom-call(s32[4]{0:T(128)S(1)} %pad_add_fusion.me_ref, ...), custom_call_target="tpu_custom_call" | custom-call | tf_op jit(solution)/shard_map/attend_forward/pallas_call | solution.py:256
  69.2 2.8 %collective-permute-done.13.refs_5_.refs_2_ = bf16[3,96,768]{2,1,0:T(8,128)(2,1)S(1)} collective-permute-done((bf16[3,96,768]{2,1,0:T(8,128)(2,1)S(1)}, bf16[3,96,768]{2,1,0:T(8,128)(2,1)S(1)}, u32[]{:S(2)}, u32[]{:S(2)}) %collective-permute-start.13) | collective-permute-done | bytes 442400 | tf_op jit(solution)/shard_map/ppermute | solution.py:659
  72.1 3.3 %collective-permute-done.14.refs_6_.refs_3_ = bf16[3,96,768]{2,1,0:T(8,128)(2,1)S(1)} collective-permute-done((bf16[3,96,768]{2,1,0:T(8,128)(2,1)S(1)}, bf16[3,96,768]{2,1,0:T(8,128)(2,1)S(1)}, u32[]{:S(2)}, u32[]{:S(2)}) %collective-permute-start.14) | collective-permute-done | bytes 442400 | tf_op jit(solution)/shard_map/ppermute | solution.py:659
  80.3 3.8 %collective-permute-done.12.refs_0_ = bf16[3,96,768]{2,1,0:T(8,128)(2,1)S(1)} collective-permute-done((bf16[3,96,768]{2,1,0:T(8,128)(2,1)S(1)}, bf16[3,96,768]{2,1,0:T(8,128)(2,1)S(1)}, u32[]{:S(2)}, u32[]{:S(2)}) %collective-permute-start.12) | collective-permute-done | bytes 442400 | tf_op jit(solution)/shard_map/ppermute | solution.py:659
  88.1 9.5 %middle_forward.1 = (bf16[512,768]{1,0:T(8,128)(2,1)}, f32[512,768]{1,0:T(8,128)S(1)}, bf16[512,768]{1,0:T(8,128)(2,1)S(1)}, bf16[3072,512]{1,0:T(8,128)(2,1)S(1...) custom-call(s32[1]{0:T(128)S(6)} %copy.123.len_ref, ...), custom_call_target="tpu_custom_call" | custom-call | tf_op jit(solution)/shard_map/middle_forward/pallas_call | solution.py:434
  97.6 3.5 %weight_grad_outer.1 = (bf16[4,4,96,768]{3,2,1,0:T(8,128)(2,1)S(1)}, bf16[4,4,96,768]{3,2,1,0:T(8,128)(2,1)S(1)}) custom-call(s32[4]{0:T(128)S(1)} %pad_add_fusion.me_ref, bf16[3072,512]{1,0:T(8,128)(2,1)S(1)} %get-tuple-element.94.left_ref, bf16[512,768]{1,0:T(8,128)(2,1)S(1)} %get-tuple-element.93.g_ref.refs_0_), custom_call_target="tpu_custom_call" | custom-call | tf_op jit(solution)/shard_map/weight_grad_outer/pallas_call | solution.py:585
  101.3 6.9 %middle_backward.1 = (bf16[4,512,768]{2,1,0:T(8,128)(2,1)S(1)}, f32[512,768]{1,0:T(8,128)S(1)}, bf16[512,768]{1,0:T(8,128)(2,1)S(1)}, bf16[512,768]{1,0:T(8,128)...) custom-call(bf16[512,768]{1,0:T(8,128)(2,1)S(1)} %after.50.low_ref, f32[512,768]{1,0:T(8,128)S(1)} %get-tuple-element.96.ssg_ref, ...), custom_call_target="tpu_custom_call" | custom-call | tf_op jit(solution)/shard_map/middle_backward/pallas_call | solution.py:494
  108.5 3.3 %weight_grad_inner.1 = (bf16[4,4,96,768]{3,2,1,0:T(8,128)(2,1)S(1)}, bf16[4,4,96,768]{3,2,1,0:T(8,128)(2,1)S(1)}) custom-call(s32[4]{0:T(128)S(1)} %pad_add_fusion.me_ref, bf16[768,512]{1,0:T(8,128)(2,1)S(1)} %get-tuple-element.101.left_ref, bf16[4,512,768]{2,1,0:T(8,128)(2,1)S(1)} %after.52.g_ref), custom_call_target="tpu_custom_call" | custom-call | tf_op jit(solution)/shard_map/weight_grad_inner/pallas_call | solution.py:585
  113.6 3.6 %attend_backward.2 = (bf16[4,512,768]{2,1,0:T(8,128)(2,1)S(1)}, f32[8,768]{1,0:T(8,128)S(1)}) custom-call(s32[1]{0:T(128)S(6)} %copy.123.len_ref, bf16[512,768]{1,0:T(8,128)(2,1)S(1)} %get-tuple-element.90.q_ref, bf16[512,768]{1,0:T(8,128)(2,1)S(1)} %get-tuple-element.91.k_ref, bf16[512,768]{1,0:T(8,128)(2,1)S(1)} %get-tuple-element.92.v_ref, ...), custom_call_target="tpu_custom_call" | custom-call | tf_op jit(solution)/shard_map/attend_backward/pallas_call | solution.py:316
  120.5 7.2 %attend_backward.3 = (bf16[4,512,768]{2,1,0:T(8,128)(2,1)S(1)}, f32[8,768]{1,0:T(8,128)S(1)}) custom-call(s32[1]{0:T(128)S(6)} %copy.123.len_ref, bf16[512,768]{1,0:T(8,128)(2,1)S(1)} %get-tuple-element.90.q_ref, bf16[512,768]{1,0:T(8,128)(2,1)S(1)} %get-tuple-element.91.k_ref, ...), custom_call_target="tpu_custom_call", output_to_operand_aliasing={{0}: (7, {}), {1}: (8, {})} | custom-call | tf_op jit(solution)/shard_map/attend_backward/pallas_call | solution.py:316
  127.7 3.4 %weight_grad_attend.1 = (bf16[4,4,104,768]{3,2,1,0:T(8,128)(2,1)S(1)}, bf16[4,4,104,768]{3,2,1,0:T(8,128)(2,1)S(1)}) custom-call(s32[4]{0:T(128)S(1)} %pad_add_fusion.me_ref, bf16[2,768,512]{2,1,0:T(8,128)(2,1)S(1)} %get-tuple-element.116.left_ref, bf16[4,512,768]{2,1,0:T(8,128)(2,1)S(1)} %get-tuple-element.114.g_ref, ...), custom_call_target="tpu_custom_call" | custom-call | tf_op jit(solution)/shard_map/weight_grad_attend/pallas_call | solution.py:585
  132.6 3.2 %input_grad.1 = (f32[512,768]{1,0:T(8,128)}, f32[8,128]{1,0:T(8,128)S(1)}) custom-call(bf16[4,512,768]{2,1,0:T(8,128)(2,1)S(1)} %get-tuple-element.114.g_ref, f32[512,768]{1,0:T(8,128)S(1)} %after.58.fsg_ref, bf16[4,768,768]{2,1,0:T(8,128)(2,1)S(1)} %get-tuple-element.88.wa.w_ref), custom_call_target="tpu_custom_call" | custom-call | tf_op jit(solution)/shard_map/input_grad/pallas_call | solution.py:530
  135.8 5.5 %collective-permute-done.26.refs_0_ = bf16[2,4,48,768]{3,2,1,0:T(8,128)(2,1)S(1)} collective-permute-done((bf16[2,4,48,768]{3,2,1,0:T(8,128)(2,1)S(1)}, bf16[2,4,48,768]{3,2,1,0:T(8,128)(2,1)S(1)}, u32[]{:S(2)}, u32[]{:S(2)}) %collective-permute-start.26) | collective-permute-done | bytes 589856 | tf_op jit(solution)/shard_map/ppermute | solution.py:659
  150.1 4.2 %collective-permute-done.32.refs_0_ = bf16[4,48,768]{2,1,0:T(8,128)(2,1)S(1)} collective-permute-done((bf16[4,48,768]{2,1,0:T(8,128)(2,1)S(1)}, bf16[4,48,768]{2,1,0:T(8,128)(2,1)S(1)}, u32[]{:S(2)}, u32[]{:S(2)}) %collective-permute-start.32) | collective-permute-done | bytes 294944 | tf_op jit(solution)/shard_map/ppermute | solution.py:659
  154.6 5.2 %collective-permute-done.30.refs_0_ = bf16[2,96,768]{2,1,0:T(8,128)(2,1)S(1)} collective-permute-done((bf16[2,96,768]{2,1,0:T(8,128)(2,1)S(1)}, bf16[2,96,768]{2,1,0:T(8,128)(2,1)S(1)}, u32[]{:S(2)}, u32[]{:S(2)}) %collective-permute-start.30) | collective-permute-done | bytes 294944 | tf_op jit(solution)/shard_map/ppermute | solution.py:659
  161.1 4.7 %collective-permute-done.27.refs_0_ = bf16[2,4,48,768]{3,2,1,0:T(8,128)(2,1)S(1)} collective-permute-done((bf16[2,4,48,768]{3,2,1,0:T(8,128)(2,1)S(1)}, bf16[2,4,48,768]{3,2,1,0:T(8,128)(2,1)S(1)}, u32[]{:S(2)}, u32[]{:S(2)}) %collective-permute-start.27) | collective-permute-done | bytes 589856 | tf_op jit(solution)/shard_map/ppermute | solution.py:659
  171.7 6.1 %collective-permute-done.36.refs_0_ = bf16[96,768]{1,0:T(8,128)(2,1)S(1)} collective-permute-done((bf16[96,768]{1,0:T(8,128)(2,1)S(1)}, bf16[96,768]{1,0:T(8,128)(2,1)S(1)}, u32[]{:S(2)}, u32[]{:S(2)}) %collective-permute-start.36) | collective-permute-done | bytes 147488 | tf_op jit(solution)/shard_map/ppermute | solution.py:659
  185.5 2.8 %collective-permute-done.39.refs_0_ = bf16[104,768]{1,0:T(8,128)(2,1)S(1)} collective-permute-done((bf16[104,768]{1,0:T(8,128)(2,1)S(1)}, bf16[104,768]{1,0:T(8,128)(2,1)S(1)}, u32[]{:S(2)}, u32[]{:S(2)}) %collective-permute-start.39) | collective-permute-done | bytes 159776 | tf_op jit(solution)/shard_map/ppermute | solution.py:659
  188.7 6.4 %collective-permute-done.40.refs_2_ = bf16[104,768]{1,0:T(8,128)(2,1)S(1)} collective-permute-done((bf16[104,768]{1,0:T(8,128)(2,1)S(1)}, bf16[104,768]{1,0:T(8,128)(2,1)S(1)}, u32[]{:S(2)}, u32[]{:S(2)}) %collective-permute-start.40) | collective-permute-done | bytes 159776 | tf_op jit(solution)/shard_map/ppermute | solution.py:659
  (164 shorter events, 72.3 us)
Async XLA Ops:
  14.1 15.1 %collective-permute-start.2 = (bf16[2,104,768]{2,1,0:T(8,128)(2,1)S(1)}, bf16[2,104,768]{2,1,0:T(8,128)(2,1)S(1)}, u32[]{:S(2)}, u32[]{:S(2)}) collective-permute-start(bf16[2,104,768]{2,1,0:T(8,128)(2,1)S(1)} %stack.21), channel_id=1, source_target_pairs={{0,2},{1,3},{2,0},{3,1},{4,6},{5,7},{6,4},{7,5},{8,10},{9,11},{10,... | collective-permute-start | bytes 958472 | tf_op jit(solution)/shard_map/ppermute | solution.py:659
  14.9 17.2 %collective-permute-start = (bf16[192,768]{1,0:T(8,128)(2,1)S(1)}, bf16[192,768]{1,0:T(8,128)(2,1)S(1)}, u32[]{:S(2)}, u32[]{:S(2)}) collective-permute-start(bf16[192,768]{1,0:T(8,128)(2,1)S(1)} %get-tuple-element.83.refs_0_), channel_id=1, source_target_pairs={{0,4},{1,5},{2,6},{3,7},{4,0},{5,1},{6,2},{7,3},{8,12},{9,13},{10,... | collective-permute-start | bytes 884744 | tf_op jit(solution)/shard_map/ppermute | solution.py:659
  32.1 13.3 %collective-permute-start.3 = (bf16[2,192,768]{2,1,0:T(8,128)(2,1)S(1)}, bf16[2,192,768]{2,1,0:T(8,128)(2,1)S(1)}, u32[]{:S(2)}, u32[]{:S(2)}) collective-permute-start(bf16[2,192,768]{2,1,0:T(8,128)(2,1)S(1)} %stack.23), channel_id=1, source_target_pairs={{0,2},{1,3},{2,0},{3,1},{4,6},{5,7},{6,4},{7,5},{8,10},{9,11},{10,... | collective-permute-start | bytes 1769480 | tf_op jit(solution)/shard_map/ppermute | solution.py:659
  49.2 17.6 %collective-permute-start.11 = (bf16[3,96,768]{2,1,0:T(8,128)(2,1)S(1)}, bf16[3,96,768]{2,1,0:T(8,128)(2,1)S(1)}, u32[]{:S(2)}, u32[]{:S(2)}) collective-permute-start(bf16[3,96,768]{2,1,0:T(8,128)(2,1)S(1)} %stack.24.refs_1_.refs_2_), channel_id=1, source_target_pairs={{0,8},{8,0},{16,24},{24,16},{1,9},{9,1},{17,25},{25,17},{2,10},{10... | collective-permute-start | bytes 1327112 | tf_op jit(solution)/shard_map/ppermute | solution.py:659
  52.8 16.1 %collective-permute-start.15 = (bf16[3,96,768]{2,1,0:T(8,128)(2,1)S(1)}, bf16[3,96,768]{2,1,0:T(8,128)(2,1)S(1)}, u32[]{:S(2)}, u32[]{:S(2)}) collective-permute-start(bf16[3,96,768]{2,1,0:T(8,128)(2,1)S(1)} %stack.25.refs_3_.refs_1_), channel_id=1, source_target_pairs={{0,16},{8,24},{16,0},{24,8},{1,17},{9,25},{17,1},{25,9},{2,18},{10... | collective-permute-start | bytes 1327112 | tf_op jit(solution)/shard_map/ppermute | solution.py:659
  53.6 18.5 %collective-permute-start.13 = (bf16[3,96,768]{2,1,0:T(8,128)(2,1)S(1)}, bf16[3,96,768]{2,1,0:T(8,128)(2,1)S(1)}, u32[]{:S(2)}, u32[]{:S(2)}) collective-permute-start(bf16[3,96,768]{2,1,0:T(8,128)(2,1)S(1)} %stack.25.refs_3_.refs_1_), channel_id=1, source_target_pairs={{0,8},{8,0},{16,24},{24,16},{1,9},{9,1},{17,25},{25,17},{2,10},{10... | collective-permute-start | bytes 1327112 | tf_op jit(solution)/shard_map/ppermute | solution.py:659
  55.9 19.5 %collective-permute-start.14 = (bf16[3,96,768]{2,1,0:T(8,128)(2,1)S(1)}, bf16[3,96,768]{2,1,0:T(8,128)(2,1)S(1)}, u32[]{:S(2)}, u32[]{:S(2)}) collective-permute-start(bf16[3,96,768]{2,1,0:T(8,128)(2,1)S(1)} %stack.24.refs_1_.refs_2_), channel_id=1, source_target_pairs={{0,16},{8,24},{16,0},{24,8},{1,17},{9,25},{17,1},{25,9},{2,18},{10... | collective-permute-start | bytes 1327112 | tf_op jit(solution)/shard_map/ppermute | solution.py:659
  66.8 17.3 %collective-permute-start.12 = (bf16[3,96,768]{2,1,0:T(8,128)(2,1)S(1)}, bf16[3,96,768]{2,1,0:T(8,128)(2,1)S(1)}, u32[]{:S(2)}, u32[]{:S(2)}) collective-permute-start(bf16[3,96,768]{2,1,0:T(8,128)(2,1)S(1)} %after.44.refs_4_.refs_2_), channel_id=1, source_target_pairs={{0,16},{8,24},{16,0},{24,8},{1,17},{9,25},{17,1},{25,9},{2,18},{10... | collective-permute-start | bytes 1327112 | tf_op jit(solution)/shard_map/ppermute | solution.py:659
  68.9 15.2 %collective-permute-start.18 = (bf16[3,96,768]{2,1,0:T(8,128)(2,1)S(1)}, bf16[3,96,768]{2,1,0:T(8,128)(2,1)S(1)}, u32[]{:S(2)}, u32[]{:S(2)}) collective-permute-start(bf16[3,96,768]{2,1,0:T(8,128)(2,1)S(1)} %after.45.refs_7_.refs_3_), channel_id=1, source_target_pairs={{0,8},{8,0},{16,24},{24,16},{1,9},{9,1},{17,25},{25,17},{2,10},{10... | collective-permute-start | bytes 1327112 | tf_op jit(solution)/shard_map/ppermute | solution.py:659
  112.4 18.7 %collective-permute-start.23 = (bf16[2,4,48,768]{3,2,1,0:T(8,128)(2,1)S(1)}, bf16[2,4,48,768]{3,2,1,0:T(8,128)(2,1)S(1)}, u32[]{:S(2)}, u32[]{:S(2)}) collective-permute-start(bf16[2,4,48,768]{3,2,1,0:T(8,128)(2,1)S(1)} %get-tuple-element.105.refs_2_), channel_id=1, source_target_pairs={{0,16},{8,24},{16,0},{24,8},{1,17},{9,25},{17,1},{25,9},{2,18},{10... | collective-permute-start | bytes 1769480 | tf_op jit(solution)/shard_map/ppermute | solution.py:659
  112.8 18.4 %collective-permute-start.22 = (bf16[2,4,48,768]{3,2,1,0:T(8,128)(2,1)S(1)}, bf16[2,4,48,768]{3,2,1,0:T(8,128)(2,1)S(1)}, u32[]{:S(2)}, u32[]{:S(2)}) collective-permute-start(bf16[2,4,48,768]{3,2,1,0:T(8,128)(2,1)S(1)} %get-tuple-element.104.refs_1_), channel_id=1, source_target_pairs={{0,8},{8,0},{16,24},{24,16},{1,9},{9,1},{17,25},{25,17},{2,10},{10... | collective-permute-start | bytes 1769480 | tf_op jit(solution)/shard_map/ppermute | solution.py:659
  117.5 23.8 %collective-permute-start.26 = (bf16[2,4,48,768]{3,2,1,0:T(8,128)(2,1)S(1)}, bf16[2,4,48,768]{3,2,1,0:T(8,128)(2,1)S(1)}, u32[]{:S(2)}, u32[]{:S(2)}) collective-permute-start(bf16[2,4,48,768]{3,2,1,0:T(8,128)(2,1)S(1)} %get-tuple-element.112.refs_2_), channel_id=1, source_target_pairs={{0,16},{8,24},{16,0},{24,8},{1,17},{9,25},{17,1},{25,9},{2,18},{10... | collective-permute-start | bytes 1769480 | tf_op jit(solution)/shard_map/ppermute | solution.py:659
  118.8 22.8 %collective-permute-start.25 = (bf16[2,4,48,768]{3,2,1,0:T(8,128)(2,1)S(1)}, bf16[2,4,48,768]{3,2,1,0:T(8,128)(2,1)S(1)}, u32[]{:S(2)}, u32[]{:S(2)}) collective-permute-start(bf16[2,4,48,768]{3,2,1,0:T(8,128)(2,1)S(1)} %get-tuple-element.111.refs_1_), channel_id=1, source_target_pairs={{0,8},{8,0},{16,24},{24,16},{1,9},{9,1},{17,25},{25,17},{2,10},{10... | collective-permute-start | bytes 1769480 | tf_op jit(solution)/shard_map/ppermute | solution.py:659
  131.4 18.2 %collective-permute-start.28 = (bf16[4,48,768]{2,1,0:T(8,128)(2,1)S(1)}, bf16[4,48,768]{2,1,0:T(8,128)(2,1)S(1)}, u32[]{:S(2)}, u32[]{:S(2)}) collective-permute-start(bf16[4,48,768]{2,1,0:T(8,128)(2,1)S(1)} %get-tuple-element.122.refs_1_), channel_id=1, source_target_pairs={{0,16},{8,24},{16,0},{24,8},{1,17},{9,25},{17,1},{25,9},{2,18},{10... | collective-permute-start | bytes 884744 | tf_op jit(solution)/shard_map/ppermute | solution.py:659
  131.8 16.1 %collective-permute-start.29 = (bf16[4,48,768]{2,1,0:T(8,128)(2,1)S(1)}, bf16[4,48,768]{2,1,0:T(8,128)(2,1)S(1)}, u32[]{:S(2)}, u32[]{:S(2)}) collective-permute-start(bf16[4,48,768]{2,1,0:T(8,128)(2,1)S(1)} %get-tuple-element.123.refs_2_), channel_id=1, source_target_pairs={{0,8},{8,0},{16,24},{24,16},{1,9},{9,1},{17,25},{25,17},{2,10},{10... | collective-permute-start | bytes 884744 | tf_op jit(solution)/shard_map/ppermute | solution.py:659
  141.9 12.4 %collective-permute-start.32 = (bf16[4,48,768]{2,1,0:T(8,128)(2,1)S(1)}, bf16[4,48,768]{2,1,0:T(8,128)(2,1)S(1)}, u32[]{:S(2)}, u32[]{:S(2)}) collective-permute-start(bf16[4,48,768]{2,1,0:T(8,128)(2,1)S(1)} %get-tuple-element.128.refs_2_), channel_id=1, source_target_pairs={{0,8},{8,0},{16,24},{24,16},{1,9},{9,1},{17,25},{25,17},{2,10},{10... | collective-permute-start | bytes 884744 | tf_op jit(solution)/shard_map/ppermute | solution.py:659
  144.3 21.4 %collective-permute-start.27 = (bf16[2,4,48,768]{3,2,1,0:T(8,128)(2,1)S(1)}, bf16[2,4,48,768]{3,2,1,0:T(8,128)(2,1)S(1)}, u32[]{:S(2)}, u32[]{:S(2)}) collective-permute-start(bf16[2,4,48,768]{3,2,1,0:T(8,128)(2,1)S(1)} %get-tuple-element.129.refs_1_), channel_id=1, source_target_pairs={{0,8},{8,0},{16,24},{24,16},{1,9},{9,1},{17,25},{25,17},{2,10},{10... | collective-permute-start | bytes 1769480 | tf_op jit(solution)/shard_map/ppermute | solution.py:659
  147.9 19.9 %collective-permute-start.33 = (bf16[2,4,56,768]{3,2,1,0:T(8,128)(2,1)S(1)}, bf16[2,4,56,768]{3,2,1,0:T(8,128)(2,1)S(1)}, u32[]{:S(2)}, u32[]{:S(2)}) collective-permute-start(bf16[2,4,56,768]{3,2,1,0:T(8,128)(2,1)S(1)} %get-tuple-element.130.refs_2_), channel_id=1, source_target_pairs={{0,16},{8,24},{16,0},{24,8},{1,17},{9,25},{17,1},{25,9},{2,18},{10... | collective-permute-start | bytes 2064392 | tf_op jit(solution)/shard_map/ppermute | solution.py:659
  154.6 14.7 %collective-permute-start.35 = (bf16[2,96,768]{2,1,0:T(8,128)(2,1)S(1)}, bf16[2,96,768]{2,1,0:T(8,128)(2,1)S(1)}, u32[]{:S(2)}, u32[]{:S(2)}) collective-permute-start(bf16[2,96,768]{2,1,0:T(8,128)(2,1)S(1)} %get-tuple-element.135), channel_id=1, source_target_pairs={{0,2},{1,3},{2,0},{3,1},{4,6},{5,7},{6,4},{7,5},{8,10},{9,11},{10,... | collective-permute-start | bytes 884744 | tf_op jit(solution)/shard_map/ppermute | solution.py:659
  159.9 11.7 %collective-permute-start.37 = (bf16[96,768]{1,0:T(8,128)(2,1)S(1)}, bf16[96,768]{1,0:T(8,128)(2,1)S(1)}, u32[]{:S(2)}, u32[]{:S(2)}) collective-permute-start(bf16[96,768]{1,0:T(8,128)(2,1)S(1)} %combine.25.refs_1_), channel_id=1, source_target_pairs={{0,4},{1,5},{2,6},{3,7},{4,0},{5,1},{6,2},{7,3},{8,12},{9,13},{10,... | collective-permute-start | bytes 442376 | tf_op jit(solution)/shard_map/ppermute | solution.py:659
  178.3 18.9 %collective-permute-start.47 = (bf16[192,768]{1,0:T(8,128)(2,1)S(1)}, bf16[192,768]{1,0:T(8,128)(2,1)S(1)}, u32[]{:S(2)}, u32[]{:S(2)}) collective-permute-start(bf16[192,768]{1,0:T(8,128)(2,1)S(1)} %combine.31.refs_1_.refs_0_), channel_id=1, source_target_pairs={{0,24},{8,16},{16,8},{24,0},{1,25},{9,17},{17,9},{25,1},{2,26},{10... | collective-permute-start | bytes 884744 | tf_op jit(solution)/shard_map/ppermute | solution.py:659
  180.8 14.4 %collective-permute-start.40 = (bf16[104,768]{1,0:T(8,128)(2,1)S(1)}, bf16[104,768]{1,0:T(8,128)(2,1)S(1)}, u32[]{:S(2)}, u32[]{:S(2)}) collective-permute-start(bf16[104,768]{1,0:T(8,128)(2,1)S(1)} %get-tuple-element.139), channel_id=1, source_target_pairs={{0,4},{1,5},{2,6},{3,7},{4,0},{5,1},{6,2},{7,3},{8,12},{9,13},{10,... | collective-permute-start | bytes 479240 | tf_op jit(solution)/shard_map/ppermute | solution.py:659
  183.4 11.8 %collective-permute-start.41 = (bf16[104,768]{1,0:T(8,128)(2,1)S(1)}, bf16[104,768]{1,0:T(8,128)(2,1)S(1)}, u32[]{:S(2)}, u32[]{:S(2)}) collective-permute-start(bf16[104,768]{1,0:T(8,128)(2,1)S(1)} %get-tuple-element.140), channel_id=1, source_target_pairs={{0,6},{1,7},{2,4},{3,5},{4,2},{5,3},{6,0},{7,1},{8,14},{9,15},{10,... | collective-permute-start | bytes 479240 | tf_op jit(solution)/shard_map/ppermute | solution.py:659
  185.1 14.8 %collective-permute-start.46 = (bf16[192,768]{1,0:T(8,128)(2,1)S(1)}, bf16[192,768]{1,0:T(8,128)(2,1)S(1)}, u32[]{:S(2)}, u32[]{:S(2)}) collective-permute-start(bf16[192,768]{1,0:T(8,128)(2,1)S(1)} %combine.31.refs_1_.refs_0_), channel_id=1, source_target_pairs={{0,16},{8,24},{16,0},{24,8},{1,17},{9,25},{17,1},{25,9},{2,18},{10... | collective-permute-start | bytes 884744 | tf_op jit(solution)/shard_map/ppermute | solution.py:659
  (27 other events, 186.6 us)

commit v2 on v1

--- a/solution.py
+++ b/solution.py
@@ -241,7 +241,7 @@
             top = jnp.max(s, axis=0, keepdims=True)
             p_t = jnp.exp(s - top)
             total = jnp.sum(p_t, axis=0, keepdims=True)
-            o_t = dot_nn(v_t[e * HD : (e + 1) * HD, :], p_t.astype(BF16)) / total
+            o_t = dot_nn(v_t[e * HD : (e + 1) * HD, :], p_t.astype(BF16)) * (1.0 / total)
             left_ref[1, aligned(p * 128 + e * HD, HD), :] = o_t.astype(BF16)
             lse_ref[pl.ds(p * 2 + e, 1), :] = top + jnp.log(total)
         att_ref[:, lanes] = flip(left_ref[1, aligned(p * 128, 128), :])
@@ -556,20 +556,25 @@
             extra[f, :, :part] = every[:, f * part : (f + 1) * part]
             extra[f, 0:1, 128 : 128 + 4 * part] = ib[f // 2 : f // 2 + 1, f % 2 * 4 * part : (f % 2 + 1) * 4 * part]
 
+    def gather(place, row_of, *lead):
+        for side, c_at in enumerate((1 - c, c)):
+            for n, j in enumerate(z_order):
+                rows = left_ref[(*lead, aligned_rows(row_of(2 * (z ^ j) + c_at), 96), slice(None))]
+                left[place, side * 384 + n * 96 : side * 384 + (n + 1) * 96, :] = rows
+
+    if kind == "inner":
+        gather(0, lambda f_at: f_at * 96)
+    elif kind == "attend":
+        gather(0, lambda f_at: f_at * 96, 0)
+        gather(1, lambda f_at: f_at * 96, 1)
+
     def block_step(spot, carry):
         block = i ^ pick(order, spot)
-        for side, c_at in enumerate((1 - c, c)):
-            for n, j in enumerate(z_order):
-                f_at = 2 * (z ^ j) + c_at
-                if kind == "outer":
-                    rows = left_ref[aligned_rows(f_at * 384 + block * 96, 96), :]
-                elif kind == "inner":
-                    rows = left_ref[aligned_rows(f_at * 96, 96), :]
-                else:
-                    rows = left_ref[block // 3, aligned_rows(f_at * 96, 96), :]
-                left[side * 384 + n * 96 : side * 384 + (n + 1) * 96, :] = rows
+        if kind == "outer":
+            gather(0, lambda f_at: f_at * 384 + block * 96)
         right = g_ref[...] if kind == "outer" else g_ref[block]
-        grads = dot_nn(left[...], right).reshape(2, 4, 96, 768).astype(BF16)
+        rows = left[block // 3] if kind == "attend" else left[0]
+        grads = dot_nn(rows, right).reshape(2, 4, 96, 768).astype(BF16)
         for side, c_at in enumerate((1 - c, c)):
             outs[side][spot, :, :96, :] = grads[side]
             if kind == "attend":
@@ -587,7 +592,7 @@
         out_shape=(local(4, 4, rows, 768),) * 2,
         in_specs=[SM] + [VM] * (2 + len(sums)),
         out_specs=[VM] * 2,
-        scratch_shapes=[pltpu.VMEM((768, left.shape[-1]), BF16)] + [pltpu.VMEM((8, 8, 768), F32)] * (kind == "attend"),
+        scratch_shapes=[pltpu.VMEM((1 + (kind == "attend"), 768, left.shape[-1]), BF16)] + [pltpu.VMEM((8, 8, 768), F32)] * (kind == "attend"),
         compiler_params=limit(6),
         cost_estimate=FREE,
         name=f"weight_grad_{kind}",

time: 205 us -> 205 us (level)
  no operation moved by 1% of the time
where the time goes in v2:
time: 205 us
  waiting for transfers between devices  81.9 us (40%)
  Pallas kernels  69.2 us (34%)
  starting transfers between devices  49.8 us (24%)
    ppermute x48, waiting for transfers between devices, swap(): return lax.ppermute(value, axis, [(n, n ^ mask) for n in range(size)])  81.9 us
    ppermute x48, starting transfers between devices, swap(): return lax.ppermute(value, axis, [(n, n ^ mask) for n in range(size)])  49.8 us
    pallas_call x1, Pallas kernels, attend_forward(): pl.pallas_call(functools.partial(attend_forward_body, group, width // sha...  10.9 us
    pallas_call x2, Pallas kernels, attend_backward(): pl.pallas_call(functools.partial(attend_backward_body, first, last), out_...  10.7 us
    pallas_call x3, Pallas kernels, weight_grad(): pl.pallas_call(functools.partial(weight_grad_body, kind, order, z_order),...  10.3 us
    pallas_call x1, Pallas kernels, middle_forward(): pl.pallas_call(middle_forward_body, out_shape=(shape(seq, width), local(s...  9.45 us
    pallas_call x1, Pallas kernels, middle_backward(): pl.pallas_call(middle_backward_body, out_shape=(local(blocks, seq, width)...  6.87 us
    pallas_call x6, Pallas kernels, fill(): pl.pallas_call(functools.partial(fill_body, group, early), out_shape=loca...  6.33 us
  transfers between devices with their start and end apart: 48, of which 22 were waited for; matrix products, arithmetic and copies ran while one was open for 1% of the time, Pallas kernels for 23%

profile of v2, /device:TPU:0, one launch (start us, length us, event | category | flops | bytes accessed | tf_op | source)
XLA Modules:
  0.0 204.6 jit_solution(2101494228132381173)
XLA Ops:
  2.5 4.1 %collective-permute-start.1 = (bf16[104,768]{1,0:T(8,128)(2,1)S(1)}, bf16[104,768]{1,0:T(8,128)(2,1)S(1)}, u32[]{:S(2)}, u32[]{:S(2)}) collective-permute-start(bf16[104,768]{1,0:T(8,128)(2,1)S(1)} %get-tuple-element.84.refs_0_.refs_7_.refs_12_), channel_id=1, source_target_pairs={{0,4},{1,5},{2,6},{3,7},{4,0},{5,1},{6,2},{7,3},{8,12},{9,13},{10,... | collective-permute-start | bytes 479240 | tf_op jit(solution)/shard_map/ppermute | solution.py:664
  6.6 7.5 %collective-permute-done.1.refs_1_ = bf16[104,768]{1,0:T(8,128)(2,1)S(1)} collective-permute-done((bf16[104,768]{1,0:T(8,128)(2,1)S(1)}, bf16[104,768]{1,0:T(8,128)(2,1)S(1)}, u32[]{:S(2)}, u32[]{:S(2)}) %collective-permute-start.1) | collective-permute-done | bytes 159776 | tf_op jit(solution)/shard_map/ppermute | solution.py:664
  14.9 3.4 %collective-permute-start = (bf16[192,768]{1,0:T(8,128)(2,1)S(1)}, bf16[192,768]{1,0:T(8,128)(2,1)S(1)}, u32[]{:S(2)}, u32[]{:S(2)}) collective-permute-start(bf16[192,768]{1,0:T(8,128)(2,1)S(1)} %get-tuple-element.83.refs_0_), channel_id=1, source_target_pairs={{0,4},{1,5},{2,6},{3,7},{4,0},{5,1},{6,2},{7,3},{8,12},{9,13},{10,... | collective-permute-start | bytes 884744 | tf_op jit(solution)/shard_map/ppermute | solution.py:664
  18.3 10.9 %collective-permute-done.2.refs_0_.refs_2_ = bf16[2,104,768]{2,1,0:T(8,128)(2,1)S(1)} collective-permute-done((bf16[2,104,768]{2,1,0:T(8,128)(2,1)S(1)}, bf16[2,104,768]{2,1,0:T(8,128)(2,1)S(1)}, u32[]{:S(2)}, u32[]{:S(2)}) %collective-permute-start.2) | collective-permute-done | bytes 319520 | tf_op jit(solution)/shard_map/ppermute | solution.py:664
  32.4 8.1 %collective-permute-done.6.refs_0_ = bf16[3,104,768]{2,1,0:T(8,128)(2,1)S(1)} collective-permute-done((bf16[3,104,768]{2,1,0:T(8,128)(2,1)S(1)}, bf16[3,104,768]{2,1,0:T(8,128)(2,1)S(1)}, u32[]{:S(2)}, u32[]{:S(2)}) %collective-permute-start.6) | collective-permute-done | bytes 479264 | tf_op jit(solution)/shard_map/ppermute | solution.py:664
  55.9 10.9 %attend_forward.1 = (bf16[512,768]{1,0:T(8,128)(2,1)S(1)}, bf16[512,768]{1,0:T(8,128)(2,1)S(1)}, bf16[512,768]{1,0:T(8,128)(2,1)S(1)}, bf16[512,768]{1,0:T(8,128...) custom-call(s32[4]{0:T(128)S(1)} %pad_add_fusion.me_ref, ...), custom_call_target="tpu_custom_call" | custom-call | tf_op jit(solution)/shard_map/attend_forward/pallas_call | solution.py:256
  69.2 2.8 %collective-permute-done.13.refs_5_.refs_2_ = bf16[3,96,768]{2,1,0:T(8,128)(2,1)S(1)} collective-permute-done((bf16[3,96,768]{2,1,0:T(8,128)(2,1)S(1)}, bf16[3,96,768]{2,1,0:T(8,128)(2,1)S(1)}, u32[]{:S(2)}, u32[]{:S(2)}) %collective-permute-start.13) | collective-permute-done | bytes 442400 | tf_op jit(solution)/shard_map/ppermute | solution.py:664
  72.1 3.3 %collective-permute-done.14.refs_6_.refs_3_ = bf16[3,96,768]{2,1,0:T(8,128)(2,1)S(1)} collective-permute-done((bf16[3,96,768]{2,1,0:T(8,128)(2,1)S(1)}, bf16[3,96,768]{2,1,0:T(8,128)(2,1)S(1)}, u32[]{:S(2)}, u32[]{:S(2)}) %collective-permute-start.14) | collective-permute-done | bytes 442400 | tf_op jit(solution)/shard_map/ppermute | solution.py:664
  80.3 3.8 %collective-permute-done.12.refs_0_ = bf16[3,96,768]{2,1,0:T(8,128)(2,1)S(1)} collective-permute-done((bf16[3,96,768]{2,1,0:T(8,128)(2,1)S(1)}, bf16[3,96,768]{2,1,0:T(8,128)(2,1)S(1)}, u32[]{:S(2)}, u32[]{:S(2)}) %collective-permute-start.12) | collective-permute-done | bytes 442400 | tf_op jit(solution)/shard_map/ppermute | solution.py:664
  88.1 9.5 %middle_forward.1 = (bf16[512,768]{1,0:T(8,128)(2,1)}, f32[512,768]{1,0:T(8,128)S(1)}, bf16[512,768]{1,0:T(8,128)(2,1)S(1)}, bf16[3072,512]{1,0:T(8,128)(2,1)S(1...) custom-call(s32[1]{0:T(128)S(6)} %copy.123.len_ref, ...), custom_call_target="tpu_custom_call" | custom-call | tf_op jit(solution)/shard_map/middle_forward/pallas_call | solution.py:434
  97.6 3.5 %weight_grad_outer.1 = (bf16[4,4,96,768]{3,2,1,0:T(8,128)(2,1)S(1)}, bf16[4,4,96,768]{3,2,1,0:T(8,128)(2,1)S(1)}) custom-call(s32[4]{0:T(128)S(1)} %pad_add_fusion.me_ref, bf16[3072,512]{1,0:T(8,128)(2,1)S(1)} %get-tuple-element.94.left_ref, bf16[512,768]{1,0:T(8,128)(2,1)S(1)} %get-tuple-element.93.g_ref.refs_0_), custom_call_target="tpu_custom_call" | custom-call | tf_op jit(solution)/shard_map/weight_grad_outer/pallas_call | solution.py:590
  101.3 6.9 %middle_backward.1 = (bf16[4,512,768]{2,1,0:T(8,128)(2,1)S(1)}, f32[512,768]{1,0:T(8,128)S(1)}, bf16[512,768]{1,0:T(8,128)(2,1)S(1)}, bf16[512,768]{1,0:T(8,128)...) custom-call(bf16[512,768]{1,0:T(8,128)(2,1)S(1)} %after.50.low_ref, f32[512,768]{1,0:T(8,128)S(1)} %get-tuple-element.96.ssg_ref, ...), custom_call_target="tpu_custom_call" | custom-call | tf_op jit(solution)/shard_map/middle_backward/pallas_call | solution.py:494
  108.5 3.4 %weight_grad_inner.1 = (bf16[4,4,96,768]{3,2,1,0:T(8,128)(2,1)S(1)}, bf16[4,4,96,768]{3,2,1,0:T(8,128)(2,1)S(1)}) custom-call(s32[4]{0:T(128)S(1)} %pad_add_fusion.me_ref, bf16[768,512]{1,0:T(8,128)(2,1)S(1)} %get-tuple-element.101.left_ref, bf16[4,512,768]{2,1,0:T(8,128)(2,1)S(1)} %after.52.g_ref), custom_call_target="tpu_custom_call" | custom-call | tf_op jit(solution)/shard_map/weight_grad_inner/pallas_call | solution.py:590
  113.6 3.6 %attend_backward.2 = (bf16[4,512,768]{2,1,0:T(8,128)(2,1)S(1)}, f32[8,768]{1,0:T(8,128)S(1)}) custom-call(s32[1]{0:T(128)S(6)} %copy.123.len_ref, bf16[512,768]{1,0:T(8,128)(2,1)S(1)} %get-tuple-element.90.q_ref, bf16[512,768]{1,0:T(8,128)(2,1)S(1)} %get-tuple-element.91.k_ref, bf16[512,768]{1,0:T(8,128)(2,1)S(1)} %get-tuple-element.92.v_ref, ...), custom_call_target="tpu_custom_call" | custom-call | tf_op jit(solution)/shard_map/attend_backward/pallas_call | solution.py:316
  120.6 7.2 %attend_backward.3 = (bf16[4,512,768]{2,1,0:T(8,128)(2,1)S(1)}, f32[8,768]{1,0:T(8,128)S(1)}) custom-call(s32[1]{0:T(128)S(6)} %copy.123.len_ref, bf16[512,768]{1,0:T(8,128)(2,1)S(1)} %get-tuple-element.90.q_ref, bf16[512,768]{1,0:T(8,128)(2,1)S(1)} %get-tuple-element.91.k_ref, ...), custom_call_target="tpu_custom_call", output_to_operand_aliasing={{0}: (7, {}), {1}: (8, {})} | custom-call | tf_op jit(solution)/shard_map/attend_backward/pallas_call | solution.py:316
  127.8 3.4 %weight_grad_attend.1 = (bf16[4,4,104,768]{3,2,1,0:T(8,128)(2,1)S(1)}, bf16[4,4,104,768]{3,2,1,0:T(8,128)(2,1)S(1)}) custom-call(s32[4]{0:T(128)S(1)} %pad_add_fusion.me_ref, bf16[2,768,512]{2,1,0:T(8,128)(2,1)S(1)} %get-tuple-element.116.left_ref, bf16[4,512,768]{2,1,0:T(8,128)(2,1)S(1)} %get-tuple-element.114.g_ref, ...), custom_call_target="tpu_custom_call" | custom-call | tf_op jit(solution)/shard_map/weight_grad_attend/pallas_call | solution.py:590
  132.7 3.2 %input_grad.1 = (f32[512,768]{1,0:T(8,128)}, f32[8,128]{1,0:T(8,128)S(1)}) custom-call(bf16[4,512,768]{2,1,0:T(8,128)(2,1)S(1)} %get-tuple-element.114.g_ref, f32[512,768]{1,0:T(8,128)S(1)} %after.58.fsg_ref, bf16[4,768,768]{2,1,0:T(8,128)(2,1)S(1)} %get-tuple-element.88.wa.w_ref), custom_call_target="tpu_custom_call" | custom-call | tf_op jit(solution)/shard_map/input_grad/pallas_call | solution.py:530
  135.9 5.4 %collective-permute-done.26.refs_0_ = bf16[2,4,48,768]{3,2,1,0:T(8,128)(2,1)S(1)} collective-permute-done((bf16[2,4,48,768]{3,2,1,0:T(8,128)(2,1)S(1)}, bf16[2,4,48,768]{3,2,1,0:T(8,128)(2,1)S(1)}, u32[]{:S(2)}, u32[]{:S(2)}) %collective-permute-start.26) | collective-permute-done | bytes 589856 | tf_op jit(solution)/shard_map/ppermute | solution.py:664
  150.1 4.2 %collective-permute-done.32.refs_0_ = bf16[4,48,768]{2,1,0:T(8,128)(2,1)S(1)} collective-permute-done((bf16[4,48,768]{2,1,0:T(8,128)(2,1)S(1)}, bf16[4,48,768]{2,1,0:T(8,128)(2,1)S(1)}, u32[]{:S(2)}, u32[]{:S(2)}) %collective-permute-start.32) | collective-permute-done | bytes 294944 | tf_op jit(solution)/shard_map/ppermute | solution.py:664
  154.7 5.2 %collective-permute-done.30.refs_0_ = bf16[2,96,768]{2,1,0:T(8,128)(2,1)S(1)} collective-permute-done((bf16[2,96,768]{2,1,0:T(8,128)(2,1)S(1)}, bf16[2,96,768]{2,1,0:T(8,128)(2,1)S(1)}, u32[]{:S(2)}, u32[]{:S(2)}) %collective-permute-start.30) | collective-permute-done | bytes 294944 | tf_op jit(solution)/shard_map/ppermute | solution.py:664
  161.1 4.7 %collective-permute-done.27.refs_0_ = bf16[2,4,48,768]{3,2,1,0:T(8,128)(2,1)S(1)} collective-permute-done((bf16[2,4,48,768]{3,2,1,0:T(8,128)(2,1)S(1)}, bf16[2,4,48,768]{3,2,1,0:T(8,128)(2,1)S(1)}, u32[]{:S(2)}, u32[]{:S(2)}) %collective-permute-start.27) | collective-permute-done | bytes 589856 | tf_op jit(solution)/shard_map/ppermute | solution.py:664
  171.7 6.1 %collective-permute-done.36.refs_0_ = bf16[96,768]{1,0:T(8,128)(2,1)S(1)} collective-permute-done((bf16[96,768]{1,0:T(8,128)(2,1)S(1)}, bf16[96,768]{1,0:T(8,128)(2,1)S(1)}, u32[]{:S(2)}, u32[]{:S(2)}) %collective-permute-start.36) | collective-permute-done | bytes 147488 | tf_op jit(solution)/shard_map/ppermute | solution.py:664
  185.6 2.8 %collective-permute-done.39.refs_0_ = bf16[104,768]{1,0:T(8,128)(2,1)S(1)} collective-permute-done((bf16[104,768]{1,0:T(8,128)(2,1)S(1)}, bf16[104,768]{1,0:T(8,128)(2,1)S(1)}, u32[]{:S(2)}, u32[]{:S(2)}) %collective-permute-start.39) | collective-permute-done | bytes 159776 | tf_op jit(solution)/shard_map/ppermute | solution.py:664
  188.8 6.5 %collective-permute-done.40.refs_2_ = bf16[104,768]{1,0:T(8,128)(2,1)S(1)} collective-permute-done((bf16[104,768]{1,0:T(8,128)(2,1)S(1)}, bf16[104,768]{1,0:T(8,128)(2,1)S(1)}, u32[]{:S(2)}, u32[]{:S(2)}) %collective-permute-start.40) | collective-permute-done | bytes 159776 | tf_op jit(solution)/shard_map/ppermute | solution.py:664
  (164 shorter events, 72.3 us)
Async XLA Ops:
  14.1 15.1 %collective-permute-start.2 = (bf16[2,104,768]{2,1,0:T(8,128)(2,1)S(1)}, bf16[2,104,768]{2,1,0:T(8,128)(2,1)S(1)}, u32[]{:S(2)}, u32[]{:S(2)}) collective-permute-start(bf16[2,104,768]{2,1,0:T(8,128)(2,1)S(1)} %stack.21), channel_id=1, source_target_pairs={{0,2},{1,3},{2,0},{3,1},{4,6},{5,7},{6,4},{7,5},{8,10},{9,11},{10,... | collective-permute-start | bytes 958472 | tf_op jit(solution)/shard_map/ppermute | solution.py:664
  14.9 17.2 %collective-permute-start = (bf16[192,768]{1,0:T(8,128)(2,1)S(1)}, bf16[192,768]{1,0:T(8,128)(2,1)S(1)}, u32[]{:S(2)}, u32[]{:S(2)}) collective-permute-start(bf16[192,768]{1,0:T(8,128)(2,1)S(1)} %get-tuple-element.83.refs_0_), channel_id=1, source_target_pairs={{0,4},{1,5},{2,6},{3,7},{4,0},{5,1},{6,2},{7,3},{8,12},{9,13},{10,... | collective-permute-start | bytes 884744 | tf_op jit(solution)/shard_map/ppermute | solution.py:664
  32.1 13.3 %collective-permute-start.3 = (bf16[2,192,768]{2,1,0:T(8,128)(2,1)S(1)}, bf16[2,192,768]{2,1,0:T(8,128)(2,1)S(1)}, u32[]{:S(2)}, u32[]{:S(2)}) collective-permute-start(bf16[2,192,768]{2,1,0:T(8,128)(2,1)S(1)} %stack.23), channel_id=1, source_target_pairs={{0,2},{1,3},{2,0},{3,1},{4,6},{5,7},{6,4},{7,5},{8,10},{9,11},{10,... | collective-permute-start | bytes 1769480 | tf_op jit(solution)/shard_map/ppermute | solution.py:664
  49.2 17.6 %collective-permute-start.11 = (bf16[3,96,768]{2,1,0:T(8,128)(2,1)S(1)}, bf16[3,96,768]{2,1,0:T(8,128)(2,1)S(1)}, u32[]{:S(2)}, u32[]{:S(2)}) collective-permute-start(bf16[3,96,768]{2,1,0:T(8,128)(2,1)S(1)} %stack.24.refs_1_.refs_2_), channel_id=1, source_target_pairs={{0,8},{8,0},{16,24},{24,16},{1,9},{9,1},{17,25},{25,17},{2,10},{10... | collective-permute-start | bytes 1327112 | tf_op jit(solution)/shard_map/ppermute | solution.py:664
  52.8 16.1 %collective-permute-start.15 = (bf16[3,96,768]{2,1,0:T(8,128)(2,1)S(1)}, bf16[3,96,768]{2,1,0:T(8,128)(2,1)S(1)}, u32[]{:S(2)}, u32[]{:S(2)}) collective-permute-start(bf16[3,96,768]{2,1,0:T(8,128)(2,1)S(1)} %stack.25.refs_3_.refs_1_), channel_id=1, source_target_pairs={{0,16},{8,24},{16,0},{24,8},{1,17},{9,25},{17,1},{25,9},{2,18},{10... | collective-permute-start | bytes 1327112 | tf_op jit(solution)/shard_map/ppermute | solution.py:664
  53.6 18.5 %collective-permute-start.13 = (bf16[3,96,768]{2,1,0:T(8,128)(2,1)S(1)}, bf16[3,96,768]{2,1,0:T(8,128)(2,1)S(1)}, u32[]{:S(2)}, u32[]{:S(2)}) collective-permute-start(bf16[3,96,768]{2,1,0:T(8,128)(2,1)S(1)} %stack.25.refs_3_.refs_1_), channel_id=1, source_target_pairs={{0,8},{8,0},{16,24},{24,16},{1,9},{9,1},{17,25},{25,17},{2,10},{10... | collective-permute-start | bytes 1327112 | tf_op jit(solution)/shard_map/ppermute | solution.py:664
  55.9 19.5 %collective-permute-start.14 = (bf16[3,96,768]{2,1,0:T(8,128)(2,1)S(1)}, bf16[3,96,768]{2,1,0:T(8,128)(2,1)S(1)}, u32[]{:S(2)}, u32[]{:S(2)}) collective-permute-start(bf16[3,96,768]{2,1,0:T(8,128)(2,1)S(1)} %stack.24.refs_1_.refs_2_), channel_id=1, source_target_pairs={{0,16},{8,24},{16,0},{24,8},{1,17},{9,25},{17,1},{25,9},{2,18},{10... | collective-permute-start | bytes 1327112 | tf_op jit(solution)/shard_map/ppermute | solution.py:664
  66.8 17.3 %collective-permute-start.12 = (bf16[3,96,768]{2,1,0:T(8,128)(2,1)S(1)}, bf16[3,96,768]{2,1,0:T(8,128)(2,1)S(1)}, u32[]{:S(2)}, u32[]{:S(2)}) collective-permute-start(bf16[3,96,768]{2,1,0:T(8,128)(2,1)S(1)} %after.44.refs_4_.refs_2_), channel_id=1, source_target_pairs={{0,16},{8,24},{16,0},{24,8},{1,17},{9,25},{17,1},{25,9},{2,18},{10... | collective-permute-start | bytes 1327112 | tf_op jit(solution)/shard_map/ppermute | solution.py:664
  68.9 15.2 %collective-permute-start.18 = (bf16[3,96,768]{2,1,0:T(8,128)(2,1)S(1)}, bf16[3,96,768]{2,1,0:T(8,128)(2,1)S(1)}, u32[]{:S(2)}, u32[]{:S(2)}) collective-permute-start(bf16[3,96,768]{2,1,0:T(8,128)(2,1)S(1)} %after.45.refs_7_.refs_3_), channel_id=1, source_target_pairs={{0,8},{8,0},{16,24},{24,16},{1,9},{9,1},{17,25},{25,17},{2,10},{10... | collective-permute-start | bytes 1327112 | tf_op jit(solution)/shard_map/ppermute | solution.py:664
  112.5 18.8 %collective-permute-start.23 = (bf16[2,4,48,768]{3,2,1,0:T(8,128)(2,1)S(1)}, bf16[2,4,48,768]{3,2,1,0:T(8,128)(2,1)S(1)}, u32[]{:S(2)}, u32[]{:S(2)}) collective-permute-start(bf16[2,4,48,768]{3,2,1,0:T(8,128)(2,1)S(1)} %get-tuple-element.105.refs_2_), channel_id=1, source_target_pairs={{0,16},{8,24},{16,0},{24,8},{1,17},{9,25},{17,1},{25,9},{2,18},{10... | collective-permute-start | bytes 1769480 | tf_op jit(solution)/shard_map/ppermute | solution.py:664
  112.8 18.4 %collective-permute-start.22 = (bf16[2,4,48,768]{3,2,1,0:T(8,128)(2,1)S(1)}, bf16[2,4,48,768]{3,2,1,0:T(8,128)(2,1)S(1)}, u32[]{:S(2)}, u32[]{:S(2)}) collective-permute-start(bf16[2,4,48,768]{3,2,1,0:T(8,128)(2,1)S(1)} %get-tuple-element.104.refs_1_), channel_id=1, source_target_pairs={{0,8},{8,0},{16,24},{24,16},{1,9},{9,1},{17,25},{25,17},{2,10},{10... | collective-permute-start | bytes 1769480 | tf_op jit(solution)/shard_map/ppermute | solution.py:664
  117.6 23.8 %collective-permute-start.26 = (bf16[2,4,48,768]{3,2,1,0:T(8,128)(2,1)S(1)}, bf16[2,4,48,768]{3,2,1,0:T(8,128)(2,1)S(1)}, u32[]{:S(2)}, u32[]{:S(2)}) collective-permute-start(bf16[2,4,48,768]{3,2,1,0:T(8,128)(2,1)S(1)} %get-tuple-element.112.refs_2_), channel_id=1, source_target_pairs={{0,16},{8,24},{16,0},{24,8},{1,17},{9,25},{17,1},{25,9},{2,18},{10... | collective-permute-start | bytes 1769480 | tf_op jit(solution)/shard_map/ppermute | solution.py:664
  118.8 22.8 %collective-permute-start.25 = (bf16[2,4,48,768]{3,2,1,0:T(8,128)(2,1)S(1)}, bf16[2,4,48,768]{3,2,1,0:T(8,128)(2,1)S(1)}, u32[]{:S(2)}, u32[]{:S(2)}) collective-permute-start(bf16[2,4,48,768]{3,2,1,0:T(8,128)(2,1)S(1)} %get-tuple-element.111.refs_1_), channel_id=1, source_target_pairs={{0,8},{8,0},{16,24},{24,16},{1,9},{9,1},{17,25},{25,17},{2,10},{10... | collective-permute-start | bytes 1769480 | tf_op jit(solution)/shard_map/ppermute | solution.py:664
  131.5 18.2 %collective-permute-start.28 = (bf16[4,48,768]{2,1,0:T(8,128)(2,1)S(1)}, bf16[4,48,768]{2,1,0:T(8,128)(2,1)S(1)}, u32[]{:S(2)}, u32[]{:S(2)}) collective-permute-start(bf16[4,48,768]{2,1,0:T(8,128)(2,1)S(1)} %get-tuple-element.122.refs_1_), channel_id=1, source_target_pairs={{0,16},{8,24},{16,0},{24,8},{1,17},{9,25},{17,1},{25,9},{2,18},{10... | collective-permute-start | bytes 884744 | tf_op jit(solution)/shard_map/ppermute | solution.py:664
  131.9 16.1 %collective-permute-start.29 = (bf16[4,48,768]{2,1,0:T(8,128)(2,1)S(1)}, bf16[4,48,768]{2,1,0:T(8,128)(2,1)S(1)}, u32[]{:S(2)}, u32[]{:S(2)}) collective-permute-start(bf16[4,48,768]{2,1,0:T(8,128)(2,1)S(1)} %get-tuple-element.123.refs_2_), channel_id=1, source_target_pairs={{0,8},{8,0},{16,24},{24,16},{1,9},{9,1},{17,25},{25,17},{2,10},{10... | collective-permute-start | bytes 884744 | tf_op jit(solution)/shard_map/ppermute | solution.py:664
  141.9 12.4 %collective-permute-start.32 = (bf16[4,48,768]{2,1,0:T(8,128)(2,1)S(1)}, bf16[4,48,768]{2,1,0:T(8,128)(2,1)S(1)}, u32[]{:S(2)}, u32[]{:S(2)}) collective-permute-start(bf16[4,48,768]{2,1,0:T(8,128)(2,1)S(1)} %get-tuple-element.128.refs_2_), channel_id=1, source_target_pairs={{0,8},{8,0},{16,24},{24,16},{1,9},{9,1},{17,25},{25,17},{2,10},{10... | collective-permute-start | bytes 884744 | tf_op jit(solution)/shard_map/ppermute | solution.py:664
  144.4 21.4 %collective-permute-start.27 = (bf16[2,4,48,768]{3,2,1,0:T(8,128)(2,1)S(1)}, bf16[2,4,48,768]{3,2,1,0:T(8,128)(2,1)S(1)}, u32[]{:S(2)}, u32[]{:S(2)}) collective-permute-start(bf16[2,4,48,768]{3,2,1,0:T(8,128)(2,1)S(1)} %get-tuple-element.129.refs_1_), channel_id=1, source_target_pairs={{0,8},{8,0},{16,24},{24,16},{1,9},{9,1},{17,25},{25,17},{2,10},{10... | collective-permute-start | bytes 1769480 | tf_op jit(solution)/shard_map/ppermute | solution.py:664
  148.0 19.9 %collective-permute-start.33 = (bf16[2,4,56,768]{3,2,1,0:T(8,128)(2,1)S(1)}, bf16[2,4,56,768]{3,2,1,0:T(8,128)(2,1)S(1)}, u32[]{:S(2)}, u32[]{:S(2)}) collective-permute-start(bf16[2,4,56,768]{3,2,1,0:T(8,128)(2,1)S(1)} %get-tuple-element.130.refs_2_), channel_id=1, source_target_pairs={{0,16},{8,24},{16,0},{24,8},{1,17},{9,25},{17,1},{25,9},{2,18},{10... | collective-permute-start | bytes 2064392 | tf_op jit(solution)/shard_map/ppermute | solution.py:664
  154.6 14.7 %collective-permute-start.35 = (bf16[2,96,768]{2,1,0:T(8,128)(2,1)S(1)}, bf16[2,96,768]{2,1,0:T(8,128)(2,1)S(1)}, u32[]{:S(2)}, u32[]{:S(2)}) collective-permute-start(bf16[2,96,768]{2,1,0:T(8,128)(2,1)S(1)} %get-tuple-element.135), channel_id=1, source_target_pairs={{0,2},{1,3},{2,0},{3,1},{4,6},{5,7},{6,4},{7,5},{8,10},{9,11},{10,... | collective-permute-start | bytes 884744 | tf_op jit(solution)/shard_map/ppermute | solution.py:664
  160.0 11.7 %collective-permute-start.37 = (bf16[96,768]{1,0:T(8,128)(2,1)S(1)}, bf16[96,768]{1,0:T(8,128)(2,1)S(1)}, u32[]{:S(2)}, u32[]{:S(2)}) collective-permute-start(bf16[96,768]{1,0:T(8,128)(2,1)S(1)} %combine.25.refs_1_), channel_id=1, source_target_pairs={{0,4},{1,5},{2,6},{3,7},{4,0},{5,1},{6,2},{7,3},{8,12},{9,13},{10,... | collective-permute-start | bytes 442376 | tf_op jit(solution)/shard_map/ppermute | solution.py:664
  178.3 18.9 %collective-permute-start.47 = (bf16[192,768]{1,0:T(8,128)(2,1)S(1)}, bf16[192,768]{1,0:T(8,128)(2,1)S(1)}, u32[]{:S(2)}, u32[]{:S(2)}) collective-permute-start(bf16[192,768]{1,0:T(8,128)(2,1)S(1)} %combine.31.refs_1_.refs_0_), channel_id=1, source_target_pairs={{0,24},{8,16},{16,8},{24,0},{1,25},{9,17},{17,9},{25,1},{2,26},{10... | collective-permute-start | bytes 884744 | tf_op jit(solution)/shard_map/ppermute | solution.py:664
  180.8 14.4 %collective-permute-start.40 = (bf16[104,768]{1,0:T(8,128)(2,1)S(1)}, bf16[104,768]{1,0:T(8,128)(2,1)S(1)}, u32[]{:S(2)}, u32[]{:S(2)}) collective-permute-start(bf16[104,768]{1,0:T(8,128)(2,1)S(1)} %get-tuple-element.139), channel_id=1, source_target_pairs={{0,4},{1,5},{2,6},{3,7},{4,0},{5,1},{6,2},{7,3},{8,12},{9,13},{10,... | collective-permute-start | bytes 479240 | tf_op jit(solution)/shard_map/ppermute | solution.py:664
  183.5 11.8 %collective-permute-start.41 = (bf16[104,768]{1,0:T(8,128)(2,1)S(1)}, bf16[104,768]{1,0:T(8,128)(2,1)S(1)}, u32[]{:S(2)}, u32[]{:S(2)}) collective-permute-start(bf16[104,768]{1,0:T(8,128)(2,1)S(1)} %get-tuple-element.140), channel_id=1, source_target_pairs={{0,6},{1,7},{2,4},{3,5},{4,2},{5,3},{6,0},{7,1},{8,14},{9,15},{10,... | collective-permute-start | bytes 479240 | tf_op jit(solution)/shard_map/ppermute | solution.py:664
  185.2 14.8 %collective-permute-start.46 = (bf16[192,768]{1,0:T(8,128)(2,1)S(1)}, bf16[192,768]{1,0:T(8,128)(2,1)S(1)}, u32[]{:S(2)}, u32[]{:S(2)}) collective-permute-start(bf16[192,768]{1,0:T(8,128)(2,1)S(1)} %combine.31.refs_1_.refs_0_), channel_id=1, source_target_pairs={{0,16},{8,24},{16,0},{24,8},{1,17},{9,25},{17,1},{25,9},{2,18},{10... | collective-permute-start | bytes 884744 | tf_op jit(solution)/shard_map/ppermute | solution.py:664
  (27 other events, 186.5 us)
